TPU v7x, 128 devices: a whole 4x4x4 slice. The times are simulated.
128 devices in a mesh: pix: 64 (over x, z, y_hi, core), col: 2 (over y_lo).
Axes of the slice: x: 4, y: 4 (y_hi: 2, y_lo: 2; y = y_hi * 2 + y_lo), z: 4, core: 2. Of those that a mesh axis runs over, the one named last changes fastest.
Arguments:
- observed: float32 [16384, 4096], P('pix', 'col'), may hold values from -40 to 40
- valid_mask: int32 [16384, 512], P('pix', 'col'), may hold values 0 or 1
- pix_factor: float32 [16384, 256], P('pix'), may hold values from -6 to 6
- col_factor: float32 [4096, 256], P('col'), may hold values from -0.375 to 0.375
Outputs:
- pix_next: float32 [16384, 256], P('pix')
- col_next: float32 [4096, 256], P('col')
- cloud: float32 [16384, 4096], P('pix', 'col')
All inputs are finite; a program needn't handle non-finite values. No bound on the sum of `valid_mask` on one device may be relied on, other than what follows from the above.
Results may differ from a plain program's by a relative error of at most 0.0003.
Values sent between devices are 32-bit elements; how exact they have to be, the bound alone decides.
A program may use at most 64 MiB of HBM per device.

v0:
```python
import jax
import jax.numpy as jnp
from jax import lax
from jax.sharding import PartitionSpec as P

BANDS = 8
WIDTH = 256
ITERS = 2
PASSES = 2


highest = lax.Precision.HIGHEST
threshold_scale = 1.0
diffusion = 0.2


def passed_along(block, axis, distance):
    devices = range(lax.axis_size(axis))
    route = [(i - distance, i) for i in devices if i - distance in devices]
    return lax.ppermute(block, axis, route)


def soft_cut(values, level):
    return jnp.sign(values) * jnp.maximum(jnp.abs(values) - level, 0.0)


def flux_of(diff, level):
    return diff / (1.0 + (diff / level) ** 2)


def level_of(residual, weight, total):
    spread = lax.psum(jnp.sum(weight * residual * residual), ("pix", "col"))
    return threshold_scale * jnp.sqrt(spread / total + 1e-06)


def smooth_pass(grid, level, strip_index, pix_count):
    has_north = strip_index > 0
    has_south = strip_index < pix_count - 1
    top_row = grid[0]
    bottom_row = grid[-1]
    north_rim = passed_along(bottom_row, "pix", 1)
    south_rim = passed_along(top_row, "pix", -1)
    north_rim = jnp.where(has_north, north_rim, top_row)
    south_rim = jnp.where(has_south, south_rim, bottom_row)
    north = jnp.concatenate([north_rim[None], grid[:-1]], axis=0)
    south = jnp.concatenate([grid[1:], south_rim[None]], axis=0)
    west = jnp.concatenate([grid[:, :1], grid[:, :-1]], axis=1)
    east = jnp.concatenate([grid[:, 1:], grid[:, -1:]], axis=1)
    summed = flux_of(north - grid, level) + flux_of(south - grid, level)
    summed = summed + flux_of(west - grid, level) + flux_of(east - grid, level)
    return grid + diffusion * summed


def per_device(observed, valid_mask, pix_factor, col_factor):
    pix_count = lax.axis_size("pix")
    col_count = lax.axis_size("col")
    pixels, columns = observed.shape
    dates = valid_mask.shape[1]
    weight = jnp.broadcast_to(
        valid_mask.astype(jnp.float32)[:, :, None], (pixels, dates, BANDS)
    ).reshape(pixels, columns)
    total = float(pixels * columns * pix_count * col_count)
    pix_fac = pix_factor
    col_fac = col_factor
    low_rank = jnp.dot(pix_fac, col_fac.T, precision=highest)
    for iteration in range(ITERS):
        residual = observed - low_rank
        level = level_of(residual, weight, total)
        sparse = weight * soft_cut(residual, level)
        misfit = weight * (sparse - residual)
        pix_grad = lax.psum(jnp.dot(misfit, col_fac, precision=highest), "col")
        change = jnp.dot(pix_grad, col_fac.T, precision=highest)
        norm_local = jnp.sum(pix_grad * pix_grad)
        curve_local = jnp.sum(weight * change * change)
        top_sum = lax.psum(norm_local, "pix")
        bottom_sum = lax.psum(curve_local, ("pix", "col"))
        step_pix = top_sum / bottom_sum
        pix_fac = pix_fac - step_pix * pix_grad
        low_rank = low_rank - step_pix * change
        misfit = weight * (sparse - (observed - low_rank))
        local_grad = lax.dot_general(
            misfit,
            pix_fac,
            (((0,), (0,)), ((), ())),
            precision=highest,
            preferred_element_type=jnp.float32,
        )
        col_grad = lax.psum(local_grad, "pix")
        shifted = jnp.dot(pix_fac, col_grad.T, precision=highest)
        norm_local = jnp.sum(col_grad * col_grad)
        curve_local = jnp.sum(weight * shifted * shifted)
        top_sum = lax.psum(norm_local, "col")
        bottom_sum = lax.psum(curve_local, ("pix", "col"))
        step_col = top_sum / bottom_sum
        col_fac = col_fac - step_col * col_grad
        low_rank = low_rank - step_col * shifted
    residual = observed - low_rank
    level = level_of(residual, weight, total)
    layer = weight * soft_cut(residual, level)
    strip_index = lax.axis_index("pix")
    grid = layer.reshape(pixels // WIDTH, WIDTH, columns)
    for sweep_index in range(PASSES):
        grid = smooth_pass(grid, level, strip_index, pix_count)
    return (pix_fac, col_fac, grid.reshape(pixels, columns))


def solution(mesh):
    in_specs = (P("pix", "col"), P("pix", "col"), P("pix", None), P("col", None))
    out_specs = (P("pix", None), P("col", None), P("pix", "col"))
    return jax.shard_map(
        per_device, mesh=mesh, in_specs=in_specs, out_specs=out_specs, check_vma=False
    )
```

profile of v0, /device:TPU:1, one launch (start us, length us, event | category | flops | bytes accessed | tf_op | source)
XLA Modules:
  0.0 2381.6 jit_solution(10405248718728174888)
XLA Ops:
  11.8 7.0 fusion
  18.7 68.7 %psum.105 = f32[]{:T(128)} all-reduce(f32[]{:T(128)} %get-tuple-element.8), channel_id=1, replica_groups=mesh['pix'=64,'col'=2] {'pix','col'}, use_global_device_ids=true, to_apply=%region_1.0 | all-reduce | flops 1 | bytes 8 | tf_op jit(solution)/shard_map/psum | solution.py:32
  88.1 5.7 fusion.20
  93.9 25.9 %all-reduce.5.cloned.1.call-done = f32[256,256]{1,0:T(8,128)} async-done(((f32[256,256]{1,0:T(8,128)}), f32[256,256]{1,0:T(8,128)}) %all-reduce.5.cloned.1.call-update) | async-done | bytes 262160 | tf_op jit(solution)/shard_map/psum | solution.py:71
  121.4 163.7 %psum.107 = f32[]{:T(128)} all-reduce(f32[]{:T(128)} %multiply_reduce_fusion.3), channel_id=1, replica_groups=mesh['pix'=64,'col'=2] {'pix'}, use_global_device_ids=true, to_apply=%region_4.0 | all-reduce | flops 1 | bytes 8 | tf_op jit(solution)/shard_map/psum | solution.py:75
  285.1 5.6 fusion.1
  290.7 68.3 %psum.108 = f32[]{:T(128)} all-reduce(f32[]{:T(128)} %get-tuple-element.19), channel_id=1, replica_groups=mesh['pix'=64,'col'=2] {'pix','col'}, use_global_device_ids=true, to_apply=%region_6.0 | all-reduce | flops 1 | bytes 8 | tf_op jit(solution)/shard_map/psum | solution.py:76
  360.4 9.0 fusion.16
  369.5 641.1 %all-reduce.7.cloned.1.call-done = f32[2048,256]{1,0:T(8,128)} async-done(((f32[2048,256]{1,0:T(8,128)}), f32[2048,256]{1,0:T(8,128)}) %all-reduce.7.cloned.1.call-update) | async-done | bytes 2097168 | tf_op jit(solution)/shard_map/psum | solution.py:88
  1013.3 4.4 psum.110
  1017.7 5.5 fusion.2
  1023.2 66.9 %psum.111 = f32[]{:T(128)} all-reduce(f32[]{:T(128)} %get-tuple-element.21), channel_id=1, replica_groups=mesh['pix'=64,'col'=2] {'pix','col'}, use_global_device_ids=true, to_apply=%region_11.0 | all-reduce | flops 1 | bytes 8 | tf_op jit(solution)/shard_map/psum | solution.py:93
  1091.4 7.4 fusion.3
  1098.8 63.0 %psum.112 = f32[]{:T(128)} all-reduce(f32[]{:T(128)} %get-tuple-element.5), channel_id=1, replica_groups=mesh['pix'=64,'col'=2] {'pix','col'}, use_global_device_ids=true, to_apply=%region_13.0 | all-reduce | flops 1 | bytes 8 | tf_op jit(solution)/shard_map/psum | solution.py:32
  1170.1 26.7 %all-reduce.9.cloned.1.call-done = f32[256,256]{1,0:T(8,128)} async-done(((f32[256,256]{1,0:T(8,128)}), f32[256,256]{1,0:T(8,128)}) %all-reduce.9.cloned.1.call-update) | async-done | bytes 262160 | tf_op jit(solution)/shard_map/psum | solution.py:71
  1198.5 163.7 %psum.114 = f32[]{:T(128)} all-reduce(f32[]{:T(128)} %multiply_reduce_fusion.2), channel_id=1, replica_groups=mesh['pix'=64,'col'=2] {'pix'}, use_global_device_ids=true, to_apply=%region_16.0 | all-reduce | flops 1 | bytes 8 | tf_op jit(solution)/shard_map/psum | solution.py:75
  1362.2 5.6 fusion.4
  1367.7 68.3 %psum.115 = f32[]{:T(128)} all-reduce(f32[]{:T(128)} %get-tuple-element.23), channel_id=1, replica_groups=mesh['pix'=64,'col'=2] {'pix','col'}, use_global_device_ids=true, to_apply=%region_18.0 | all-reduce | flops 1 | bytes 8 | tf_op jit(solution)/shard_map/psum | solution.py:76
  1437.5 9.1 fusion.7
  1446.6 641.2 %all-reduce.11.cloned.1.call-done = f32[2048,256]{1,0:T(8,128)} async-done(((f32[2048,256]{1,0:T(8,128)}), f32[2048,256]{1,0:T(8,128)}) %all-reduce.11.cloned.1.call-update) | async-done | bytes 2097168 | tf_op jit(solution)/shard_map/psum | solution.py:88
  2090.6 4.4 psum.117
  2095.0 5.5 fusion.5
  2100.5 66.9 %psum.118 = f32[]{:T(128)} all-reduce(f32[]{:T(128)} %get-tuple-element.25), channel_id=1, replica_groups=mesh['pix'=64,'col'=2] {'pix','col'}, use_global_device_ids=true, to_apply=%region_23.0 | all-reduce | flops 1 | bytes 8 | tf_op jit(solution)/shard_map/psum | solution.py:93
  2168.6 6.5 fusion.6
  2175.1 62.9 %psum.119 = f32[]{:T(128)} all-reduce(f32[]{:T(128)} %get-tuple-element.3), channel_id=1, replica_groups=mesh['pix'=64,'col'=2] {'pix','col'}, use_global_device_ids=true, to_apply=%region_25.0 | all-reduce | flops 1 | bytes 8 | tf_op jit(solution)/shard_map/psum | solution.py:32
  2238.7 3.7 multiply_multiply_fusion.7
  2244.9 4.6 collective-permute-start
  2253.0 36.6 %collective-permute-done.1 = f32[256,2048]{1,0:T(8,128)S(1)} collective-permute-done((f32[256,2048]{1,0:T(8,128)}, f32[256,2048]{1,0:T(8,128)S(1)}, u32[]{:S(2)}, u32[]{:S(2)}) %collective-permute-start.1) | collective-permute-done | bytes 2097184 | tf_op jit(solution)/shard_map/ppermute | solution.py:20
  2289.6 27.2 %collective-permute-done = f32[256,2048]{1,0:T(8,128)} collective-permute-done((f32[256,2048]{1,0:T(8,128)}, f32[256,2048]{1,0:T(8,128)}, u32[]{:S(2)}, u32[]{:S(2)}) %collective-permute-start) | collective-permute-done | bytes 2097184 | tf_op jit(solution)/shard_map/ppermute | solution.py:20
  2316.8 4.4 multiply_add_fusion.1
  2323.1 5.9 collective-permute-start.2
  2331.1 40.4 %collective-permute-done.3 = f32[256,2048]{1,0:T(8,128)S(1)} collective-permute-done((f32[256,2048]{1,0:T(8,128)S(1)}, f32[256,2048]{1,0:T(8,128)S(1)}, u32[]{:S(2)}, u32[]{:S(2)}) %collective-permute-start.3) | collective-permute-done | bytes 2097184 | tf_op jit(solution)/shard_map/ppermute | solution.py:20
  (47 shorter events, 34.2 us)
Async XLA Ops:
  7.2 112.6 %all-reduce.5.cloned.1.call-start = ((), (), s32[]{:S(2)}) async-start(), calls=%async_computation | async-start | bytes 524288 | tf_op jit(solution)/shard_map/psum | solution.py:71
  9.8 2.0 copy-start.8
  93.8 916.7 %all-reduce.7.cloned.1.call-start = ((), (), s32[]{:S(2)}) async-start(), calls=%async_computation.1 | async-start | bytes 4194304 | tf_op jit(solution)/shard_map/psum | solution.py:88
  285.1 75.3 %copy-start.6 = (f32[256,256]{1,0:T(8,128)S(1)}, f32[256,256]{1,0:T(8,128)}, u32[]{:S(2)}) copy-start(f32[256,256]{1,0:T(8,128)} %all-reduce.5.cloned.1.call-done) | copy-start | bytes 786436
  369.4 827.5 %all-reduce.9.cloned.1.call-start = ((), (), s32[]{:S(2)}) async-start(), calls=%async_computation.2 | async-start | bytes 524288 | tf_op jit(solution)/shard_map/psum | solution.py:71
  1162.5 4.0 copy-start.3
  1165.2 1.4 copy-start
  1170.1 917.7 %all-reduce.11.cloned.1.call-start = ((), (), s32[]{:S(2)}) async-start(), calls=%async_computation.3 | async-start | bytes 4194304 | tf_op jit(solution)/shard_map/psum | solution.py:88
  1362.2 75.3 %copy-start.5 = (f32[256,256]{1,0:T(8,128)S(1)}, f32[256,256]{1,0:T(8,128)}, u32[]{:S(2)}) copy-start(f32[256,256]{1,0:T(8,128)} %all-reduce.9.cloned.1.call-done) | copy-start | bytes 786436
  1437.5 657.5 %copy-start.4 = (f32[256,256]{1,0:T(8,128)}, f32[256,256]{1,0:T(8,128)S(1)}, u32[]{:S(2)}) copy-start(f32[256,256]{1,0:T(8,128)S(1)} %multiply_subtract_fusion.7) | copy-start | bytes 786436
  2242.4 47.1 %collective-permute-start.1 = (f32[256,2048]{1,0:T(8,128)}, f32[256,2048]{1,0:T(8,128)S(1)}, u32[]{:S(2)}, u32[]{:S(2)}) collective-permute-start(f32[256,2048]{1,0:T(8,128)} %multiply_multiply_fusion.7), channel_id=1, source_target_pairs={{2,0},{4,2},{6,4},{8,6},{10,8},{12,10},{14,12},{16,14},{18,16},{20... | collective-permute-start | bytes 6291464 | tf_op jit(solution)/shard_map/ppermute | solution.py:20
  2244.9 71.9 %collective-permute-start = (f32[256,2048]{1,0:T(8,128)}, f32[256,2048]{1,0:T(8,128)}, u32[]{:S(2)}, u32[]{:S(2)}) collective-permute-start(f32[256,2048]{1,0:T(8,128)} %multiply_multiply_fusion.7), channel_id=1, source_target_pairs={{0,2},{2,4},{4,6},{6,8},{8,10},{10,12},{12,14},{14,16},{16,18},{18... | collective-permute-start | bytes 6291464 | tf_op jit(solution)/shard_map/ppermute | solution.py:20
  2289.6 27.2 %copy-start.7 = (f32[256,2048]{1,0:T(8,128)}, f32[256,2048]{1,0:T(8,128)S(1)}, u32[]{:S(2)}) copy-start(f32[256,2048]{1,0:T(8,128)S(1)} %collective-permute-done.1) | copy-start | bytes 6291460
  2316.8 12.2 copy-start.1
  2316.8 12.2 copy-start.2
  2321.2 50.3 %collective-permute-start.3 = (f32[256,2048]{1,0:T(8,128)S(1)}, f32[256,2048]{1,0:T(8,128)S(1)}, u32[]{:S(2)}, u32[]{:S(2)}) collective-permute-start(f32[256,2048]{1,0:T(8,128)S(1)} %multiply_add_fusion.1), channel_id=1, source_target_pairs={{2,0},{4,2},{6,4},{8,6},{10,8},{12,10},{14,12},{16,14},{18,16},{20... | collective-permute-start | bytes 6291464 | tf_op jit(solution)/shard_map/ppermute | solution.py:20
  2323.1 48.4 %collective-permute-start.2 = (f32[256,2048]{1,0:T(8,128)S(1)}, f32[256,2048]{1,0:T(8,128)S(1)}, u32[]{:S(2)}, u32[]{:S(2)}) collective-permute-start(f32[256,2048]{1,0:T(8,128)S(1)} %multiply_add_fusion.1), channel_id=1, source_target_pairs={{0,2},{2,4},{4,6},{6,8},{8,10},{10,12},{12,14},{14,16},{16,18},{18... | collective-permute-start | bytes 6291464 | tf_op jit(solution)/shard_map/ppermute | solution.py:20
Sparse Core Ops, SparseCore 0:
  94.0 25.7 all-reduce.4
  369.5 640.9 all-reduce.6
  1170.2 26.6 all-reduce.8
  1446.7 641.0 all-reduce.10
where the time goes:
time: 2390 us; the launch traced here: 2380 us
  waiting for transfers between devices  1440 us (60%)
  blocking collectives  801 us (34%)
  matrix products  56.5 us (2%)
  other arithmetic  39.3 us (2%)
    psum x2, waiting for transfers between devices, per_device(): col_grad = lax.psum(local_grad, 'pix')  1280 us
    psum x2, blocking collectives, per_device(): top_sum = lax.psum(norm_local, 'pix')  327 us
    psum x4, blocking collectives, per_device(): bottom_sum = lax.psum(curve_local, ('pix', 'col'))  270 us
    psum x3, blocking collectives, level_of(): spread = lax.psum(jnp.sum(weight * residual * residual), ('pix', 'col'))  195 us
    ppermute x4, waiting for transfers between devices, passed_along(): return lax.ppermute(block, axis, route)  104 us
    psum x2, waiting for transfers between devices, per_device(): pix_grad = lax.psum(jnp.dot(misfit, col_fac, precision=highest), 'col')  52.6 us
  transfers between devices with their start and end apart: 8, of which 7 were waited for; matrix products, arithmetic and copies ran while one was open for 0% of the time, Pallas kernels for 0%

commit v1 on v0

v1 whole, which is shorter than its diff:
```python
import functools

import jax
import jax.numpy as jnp
from jax import lax
from jax.experimental import pallas as pl
from jax.experimental.pallas import tpu as pltpu
from jax.sharding import PartitionSpec as P

BANDS = 8
WIDTH = 256
ITERS = 2
PASSES = 2
TILE = 256
TILES = 8
TOTAL = 67108864.0
diffusion = 0.2

f32 = jnp.float32
bf16 = jnp.bfloat16
MESH = pl.DeviceIdType.MESH


def split(x):
    hi = x.astype(bf16)
    return hi, (x - hi.astype(f32)).astype(bf16)


def mm(a, b):
    return lax.dot_general(a, b, (((1,), (0,)), ((), ())), preferred_element_type=f32)


def mm_nt(a, b):
    return lax.dot_general(a, b, (((1,), (1,)), ((), ())), preferred_element_type=f32)


def fold(x):
    part = x.reshape(x.shape[0] // 8, 8, x.shape[1]).sum(axis=0)
    return part[:, :128] + part[:, 128:]


def pack(*parts):
    rows = [jnp.sum(part, axis=0, keepdims=True) for part in parts]
    rows.append(jnp.zeros((8 - len(rows), 128), f32))
    return jnp.concatenate(rows, axis=0)


def factor_kernel(
    obs_in, mask_in, u_in, v_in,
    u_out, v_out, layer_out, level_out,
    r, w, c, vt, vs, hp, hsib, hf, vio, lay, mask, spread,
    u, us, uts, gp, gr, gs,
    f1p, f1m, n1p, n1m, f2p, f2m, n2p, n2m, ybuf,
    s1, s2, lev,
    in_sem, out_sem, ss1, rs1, ss2, rs2, gss, grs, sibs, sibr,
    r1s, r1r, r2s, r2r, ys, yr, a2s, a2r, a1s, a1r, fs, fr,
):
    p = lax.axis_index("pix")
    lo = lax.axis_index("col")
    core, h, z, x = p % 2, (p // 2) % 2, (p // 4) % 4, p // 16

    def dev(x, z, h, core, lo):
        return {"pix": ((x * 4 + z) * 2 + h) * 2 + core, "col": lo}

    i1 = (h * 2 + core) * 2 + lo
    i2 = x * 4 + z

    def peer1(d):
        j = (i1 + d) % 8
        return dev(x, z, j // 4, (j // 2) % 2, j % 2)

    def peer2(d):
        j = (i2 + d) % 16
        return dev(j // 4, j % 4, h, core, lo)

    sibling = dev(x, z, h, 1 - core, lo)
    col_pair = dev(x, z, h, core, 1 - lo)
    y_pair = dev(x, z, 1 - h, core, lo)
    q1 = x + core * (z - x)
    q2 = z + core * (x - z)

    def ring1(q):
        return dev(q + core * (x - q), z + core * (q - z), h, core, lo)

    def ring2(q):
        return dev(x + core * (q - x), q + core * (z - q), h, core, lo)

    def rcopy(src, dst, send, recv, to):
        return pltpu.make_async_remote_copy(
            src_ref=src, dst_ref=dst, send_sem=send, recv_sem=recv, device_id=to, device_id_type=MESH
        )

    barrier = pltpu.get_barrier_semaphore()
    for d in range(1, 8):
        pl.semaphore_signal(barrier, inc=1, device_id=peer1(d), device_id_type=MESH)
    for d in range(1, 16):
        pl.semaphore_signal(barrier, inc=1, device_id=peer2(d), device_id_type=MESH)

    def tile_cols(t):
        return pl.ds(pl.multiple_of(t * TILE, TILE), TILE)

    loads = [pltpu.make_async_copy(v_in.at[pl.ds(t * TILE, TILE)], vio.at[t], in_sem.at[t]) for t in range(TILES)]
    loads.append(pltpu.make_async_copy(u_in, u, in_sem.at[TILES]))
    loads.append(pltpu.make_async_copy(mask_in, mask, in_sem.at[TILES + 1]))
    for t in range(TILES):
        loads.append(
            pltpu.make_async_copy(obs_in.at[:, pl.ds(t * TILE, TILE)], r.at[t], in_sem.at[TILES + 2 + t])
        )
    for load in loads:
        load.start()
    for part in range(4):
        date = lax.broadcasted_iota(jnp.int32, (128, TILE), 0)
        column = lax.broadcasted_iota(jnp.int32, (128, TILE), 1) + part * TILE
        gap = column - date * BANDS
        spread[part] = jnp.where((gap >= 0) & (gap < BANDS), 1.0, 0.0).astype(bf16)
    for load in loads[: TILES]:
        load.wait()

    def turn_v(t, _):
        vt_t = jnp.transpose(vio[t])
        vt[t] = vt_t
        hi, low = split(vt_t)
        vs[t, 0] = hi
        vs[t, 1] = low
        return 0

    lax.fori_loop(0, TILES, turn_v, 0)
    for load in loads[TILES:]:
        load.wait()

    def set_u(value):
        u[...] = value
        hi, low = split(value)
        us[0] = hi
        us[1] = low

    set_u(u[...])

    def dot3(a_ref, hi, low):
        return mm(a_ref[0], hi) + mm(a_ref[0], low) + mm(a_ref[1], hi)

    def first(t, acc):
        dates = mask[:, pl.ds(pl.multiple_of((t // 4) * 128, 128), 128)].astype(f32).astype(bf16)
        w_t = mm(dates, spread[t % 4])
        w[t] = w_t
        r_t = w_t * (r[t] - dot3(us, vs[t, 0], vs[t, 1]))
        r[t] = r_t
        return acc + fold(r_t * r_t)

    zero = jnp.zeros((8, 128), f32)
    square = lax.fori_loop(0, TILES, first, zero)
    pl.semaphore_wait(barrier, 22)

    def all_reduce(k, message):
        s1[k, i1] = message
        for d in range(1, 8):
            rcopy(s1.at[k, i1], s1.at[k, i1], ss1.at[k], rs1.at[k], peer1(d)).start()
        whole = s1.at[k, pl.ds(0, 7)]
        done = rcopy(whole, whole, ss1.at[k], rs1.at[k], sibling)
        done.wait_recv()
        total = s1[k, 0]
        for j in range(1, 8):
            total = total + s1[k, j]
        s2[k, i2] = total
        for d in range(1, 16):
            rcopy(s2.at[k, i2], s2.at[k, i2], ss2.at[k], rs2.at[k], peer2(d)).start()
        done.wait_send()
        whole = s2.at[k, pl.ds(0, 15)]
        done = rcopy(whole, whole, ss2.at[k], rs2.at[k], ring1((q1 + 1) % 4))
        done.wait_recv()
        total = s2[k, 0]
        for j in range(1, 16):
            total = total + s2[k, j]
        done.wait_send()
        return jnp.sum(total, axis=1, keepdims=True)

    def level_from(square):
        return jnp.sqrt(jnp.maximum(square, 0.0) / TOTAL + 1e-06)

    sums = all_reduce(0, pack(square))
    lev[...] = jnp.broadcast_to(level_from(sums[0:1]), (8, 128))

    def cut(value, level):
        return jnp.minimum(jnp.maximum(value, -level), level)

    def ring_reduce(blk, rows, q, ring, fp, fm, np_, nm, sends, recvs):
        half = rows // 2
        plus, minus = ring((q + 1) % 4), ring((q + 3) % 4)
        kp, km, kf = (q + 1) % 4, (q + 3) % 4, (q + 2) % 4
        c1 = rcopy(blk(kf, 0, half), fp, sends.at[0], recvs.at[0], plus)
        c2 = rcopy(blk(kf, half, half), fm, sends.at[1], recvs.at[1], minus)
        c3 = rcopy(blk(kp, half, half), np_.at[pl.ds(half, half)], sends.at[2], recvs.at[2], plus)
        c4 = rcopy(blk(km, 0, half), nm.at[pl.ds(0, half)], sends.at[3], recvs.at[3], minus)
        for copy in (c1, c2, c3, c4):
            copy.start()
        c1.wait_recv()
        ref = blk(kp, 0, half)
        ref[...] = ref[...] + fp[...]
        c5 = rcopy(ref, np_.at[pl.ds(0, half)], sends.at[4], recvs.at[4], plus)
        c5.start()
        c2.wait_recv()
        ref = blk(km, half, half)
        ref[...] = ref[...] + fm[...]
        c6 = rcopy(ref, nm.at[pl.ds(half, half)], sends.at[5], recvs.at[5], minus)
        c6.start()
        for copy in (c3, c4, c5, c6):
            copy.wait_recv()
        ref = blk(q, 0, rows)
        ref[...] = ref[...] + np_[...] + nm[...]
        for copy in (c1, c2, c3, c4, c5, c6):
            copy.wait_send()

    def ring_gather(blk, rows, q, ring, sends, recvs, on_block):
        half = rows // 2
        plus, minus = ring((q + 1) % 4), ring((q + 3) % 4)
        kp, km, kf = (q + 1) % 4, (q + 3) % 4, (q + 2) % 4
        own = blk(q, 0, rows)
        c1 = rcopy(own, own, sends.at[0], recvs.at[0], plus)
        c2 = rcopy(own, own, sends.at[1], recvs.at[1], minus)
        c1.start()
        c2.start()
        on_block(0, blk(q, 0, rows))
        rcopy(own, blk(km, 0, rows), sends.at[0], recvs.at[0], plus).wait_recv()
        ref = blk(km, 0, half)
        c3 = rcopy(ref, ref, sends.at[2], recvs.at[2], plus)
        c3.start()
        on_block(1, blk(km, 0, rows))
        rcopy(own, blk(kp, 0, rows), sends.at[1], recvs.at[1], plus).wait_recv()
        ref = blk(kp, half, half)
        c4 = rcopy(ref, ref, sends.at[3], recvs.at[3], minus)
        c4.start()
        on_block(2, blk(kp, 0, rows))
        rcopy(ref, blk(kf, 0, half), sends.at[2], recvs.at[2], plus).wait_recv()
        rcopy(ref, blk(kf, half, half), sends.at[3], recvs.at[3], minus).wait_recv()
        on_block(3, blk(kf, 0, rows))
        for copy in (c1, c2, c3, c4):
            copy.wait_send()

    def iteration(it, _):
        level = lev[0:1, 0:1]

        copies = []
        for part in range(2):
            rows = pl.ds(part * 128, 128)

            def grow(t, acc):
                hi, low = split(cut(r[t, rows, :], level))
                v_hi, v_low = vs[t, 0], vs[t, 1]
                return acc + mm_nt(hi, v_hi) + mm_nt(hi, v_low) + mm_nt(low, v_hi)

            gp[rows, :] = lax.fori_loop(0, TILES, grow, jnp.zeros((128, TILE), f32))
            copies.append(rcopy(gp.at[rows], gr.at[rows], gss.at[part], grs.at[part], col_pair))
            copies[-1].start()
        for copy in copies:
            copy.wait()
        g = gp[...] + gr[...]
        gp[...] = g
        hi, low = split(g)
        gs[0] = hi
        gs[1] = low

        def curve(t, acc):
            c_t = w[t] * dot3(gs, vs[t, 0], vs[t, 1])
            c[t] = c_t
            return acc + fold(c_t * c_t)

        bottom = lax.fori_loop(0, TILES, curve, zero)
        sums = all_reduce(1 + 2 * it, pack(fold(g * g) * 0.5, bottom))
        step = sums[0:1] / sums[1:2]
        set_u(u[...] + step * gp[...])
        hi, low = split(jnp.transpose(u[...]))
        uts[0] = hi
        uts[1] = low

        def pull(t):
            r_t, ac = r[t], step * c[t]
            r[t] = r_t - ac
            hi, low = split(cut(r_t, level) - ac)
            hp[t] = dot3(uts, hi, low)

        first_tile = 4 * (1 - core)

        def pull_other(i, _):
            k = (q2 + 2 + i) % 4
            pull(first_tile + k)
            rcopy(hp.at[first_tile + k], hsib.at[k], sibs.at[k], sibr.at[k], sibling).start()
            return 0

        lax.fori_loop(0, 4, pull_other, 0)
        mine = 4 * core

        def pull_own(i, _):
            pull(mine + (q1 + 2 + i) % 4)
            return 0

        lax.fori_loop(0, 4, pull_own, 0)

        def join(i, _):
            k = (q1 + 2 + i) % 4
            rcopy(hp.at[first_tile + k], hsib.at[k], sibs.at[k], sibr.at[k], sibling).wait_recv()
            hp[mine + k] = hp[mine + k] + hsib[k]
            return 0

        lax.fori_loop(0, 4, join, 0)

        def blk1(k, start, rows):
            return hp.at[mine + k, pl.ds(start, rows)]

        ring_reduce(blk1, 256, q1, ring1, f1p, f1m, n1p, n1m, r1s, r1r)

        def blk2(k, start, rows):
            return hp.at[mine + q1, pl.ds(pl.multiple_of(64 * k + start, 32), rows)]

        ring_reduce(blk2, 64, q2, ring2, f2p, f2m, n2p, n2m, r2s, r2r)
        own = blk2(q2, 0, 64)
        copy = rcopy(own, ybuf, ys, yr, y_pair)
        copy.start()
        copy.wait()
        piece = own[...] + ybuf[...]
        hf[mine + q1, pl.ds(pl.multiple_of(64 * q2, 64), 64), :] = piece
        norm = fold(piece * piece) * 0.5

        def fblk2(k, start, rows):
            return hf.at[mine + q1, pl.ds(pl.multiple_of(64 * k + start, 32), rows)]

        ring_gather(fblk2, 64, q2, ring2, a2s, a2r, lambda i, ref: None)

        def fblk1(k, start, rows):
            return hf.at[mine + k, pl.ds(start, rows)]

        def hand_over(i, ref):
            rcopy(ref, ref, fs.at[i], fr.at[i], sibling).start()

        ring_gather(fblk1, 256, q1, ring1, a1s, a1r, hand_over)

        def shift(t, accs):
            hi, low = split(hf[t])
            s_t = w[t] * dot3(us, hi, low)
            c[t] = s_t
            r_t = r[t]
            a0, a1, a2 = accs
            return a0 + fold(r_t * r_t), a1 + fold(r_t * s_t), a2 + fold(s_t * s_t)

        accs = lax.fori_loop(0, 4, lambda i, accs: shift(mine + i, accs), (zero, zero, zero))
        for i in range(4):
            ref = hf.at[first_tile + i]
            wait = rcopy(ref, ref, fs.at[i], fr.at[i], sibling)
            wait.wait_recv()
        for i in range(4):
            ref = hf.at[first_tile + i]
            rcopy(ref, ref, fs.at[i], fr.at[i], sibling).wait_send()
            rcopy(hp.at[first_tile + i], hsib.at[i], sibs.at[i], sibr.at[i], sibling).wait_send()
        accs = lax.fori_loop(0, 4, lambda i, accs: shift(first_tile + i, accs), accs)
        sums = all_reduce(2 + 2 * it, pack(norm, *accs))
        step = sums[0:1] / sums[3:4]
        square = sums[1:2] - 2.0 * step * sums[2:3] + step * step * sums[3:4]
        lev[...] = jnp.broadcast_to(level_from(square), (8, 128))

        def update(t, _):
            v_t = vt[t] + step * hf[t]
            vt[t] = v_t
            hi, low = split(v_t)
            vs[t, 0] = hi
            vs[t, 1] = low
            r[t] = r[t] - step * c[t]
            return 0

        lax.fori_loop(0, TILES, update, 0)
        return 0

    lax.fori_loop(0, ITERS, iteration, 0)
    level = lev[0:1, 0:1]

    def finish(t, _):
        r_t = r[t]
        lay[t] = r_t - cut(r_t, level)
        vio[t] = jnp.transpose(vt[t])
        return 0

    lax.fori_loop(0, TILES, finish, 0)
    stores = [pltpu.make_async_copy(u, u_out, out_sem.at[0]), pltpu.make_async_copy(lev, level_out, out_sem.at[1])]
    for t in range(TILES):
        stores.append(pltpu.make_async_copy(vio.at[t], v_out.at[pl.ds(t * TILE, TILE)], out_sem.at[2 + t]))
        stores.append(
            pltpu.make_async_copy(lay.at[t], layer_out.at[:, pl.ds(t * TILE, TILE)], out_sem.at[2 + TILES + t])
        )
    for store in stores:
        store.start()
    for store in stores:
        store.wait()


def factors(observed, valid_mask, pix_factor, col_factor):
    any_space = pl.BlockSpec(memory_space=pl.ANY)
    full = pltpu.VMEM((TILES, TILE, TILE), f32)
    square = pltpu.VMEM((TILE, TILE), f32)
    dma = pltpu.SemaphoreType.DMA
    return pl.pallas_call(
        factor_kernel,
        out_shape=(
            jax.ShapeDtypeStruct((256, 256), f32),
            jax.ShapeDtypeStruct((2048, 256), f32),
            jax.ShapeDtypeStruct((256, 2048), f32),
            jax.ShapeDtypeStruct((8, 128), f32),
        ),
        in_specs=[any_space] * 4,
        out_specs=[any_space] * 4,
        scratch_shapes=[
            full, full, full, full,
            pltpu.VMEM((TILES, 2, TILE, TILE), bf16),
            full,
            pltpu.VMEM((4, TILE, TILE), f32),
            full, full, full,
            pltpu.VMEM((256, 256), jnp.int32),
            pltpu.VMEM((4, 128, TILE), bf16),
            square,
            pltpu.VMEM((2, TILE, TILE), bf16),
            pltpu.VMEM((2, TILE, TILE), bf16),
            square, square,
            pltpu.VMEM((2, TILE, TILE), bf16),
            pltpu.VMEM((128, TILE), f32), pltpu.VMEM((128, TILE), f32), square, square,
            pltpu.VMEM((32, TILE), f32), pltpu.VMEM((32, TILE), f32),
            pltpu.VMEM((64, TILE), f32), pltpu.VMEM((64, TILE), f32),
            pltpu.VMEM((64, TILE), f32),
            pltpu.VMEM((5, 8, 8, 128), f32),
            pltpu.VMEM((5, 16, 8, 128), f32),
            pltpu.VMEM((8, 128), f32),
            dma((2 * TILES + 2,)), dma((2 * TILES + 2,)),
            dma((5,)), dma((5,)), dma((5,)), dma((5,)),
            dma((2,)), dma((2,)), dma((4,)), dma((4,)),
            dma((6,)), dma((6,)), dma((6,)), dma((6,)), dma, dma,
            dma((4,)), dma((4,)), dma((4,)), dma((4,)), dma((4,)), dma((4,)),
        ],
        compiler_params=pltpu.CompilerParams(
            collective_id=0, has_side_effects=True, vmem_limit_bytes=56 * 1024 * 1024
        ),
        name="factors",
    )(observed, valid_mask, pix_factor, col_factor)


def passed_along(block, axis, distance):
    devices = range(lax.axis_size(axis))
    route = [(i - distance, i) for i in devices if i - distance in devices]
    return lax.ppermute(block, axis, route)


def flux_of(diff, level):
    return diff / (1.0 + (diff / level) ** 2)


def smooth_pass(grid, level, strip_index, pix_count):
    has_north = strip_index > 0
    has_south = strip_index < pix_count - 1
    top_row = grid[0]
    bottom_row = grid[-1]
    north_rim = passed_along(bottom_row, "pix", 1)
    south_rim = passed_along(top_row, "pix", -1)
    north_rim = jnp.where(has_north, north_rim, top_row)
    south_rim = jnp.where(has_south, south_rim, bottom_row)
    north = jnp.concatenate([north_rim[None], grid[:-1]], axis=0)
    south = jnp.concatenate([grid[1:], south_rim[None]], axis=0)
    west = jnp.concatenate([grid[:, :1], grid[:, :-1]], axis=1)
    east = jnp.concatenate([grid[:, 1:], grid[:, -1:]], axis=1)
    summed = flux_of(north - grid, level) + flux_of(south - grid, level)
    summed = summed + flux_of(west - grid, level) + flux_of(east - grid, level)
    return grid + diffusion * summed


def per_device(observed, valid_mask, pix_factor, col_factor):
    pix_fac, col_fac, layer, level = factors(observed, valid_mask, pix_factor, col_factor)
    level = level[0, 0]
    pixels, columns = observed.shape
    strip_index = lax.axis_index("pix")
    grid = layer.reshape(pixels // WIDTH, WIDTH, columns)
    for sweep_index in range(PASSES):
        grid = smooth_pass(grid, level, strip_index, lax.axis_size("pix"))
    return (pix_fac, col_fac, grid.reshape(pixels, columns))


def solution(mesh):
    in_specs = (P("pix", "col"), P("pix", "col"), P("pix", None), P("col", None))
    out_specs = (P("pix", None), P("col", None), P("pix", "col"))
    return jax.shard_map(
        per_device, mesh=mesh, in_specs=in_specs, out_specs=out_specs, check_vma=False
    )
```

time: 2390 us -> 304 us (0.13)
  waiting for transfers between devices: 1440 us -> 103 us
  blocking collectives: 801 us -> 0 us
  Pallas kernels: 0 us -> 169 us
  matrix products: 56.5 us -> 0 us
  other arithmetic: 39.3 us -> 8.39 us
    psum x4 -> x0, waiting for transfers between devices: 1330 us -> none  [the longest x2 1280 us: per_device(): col_grad = lax.psum(local_grad, 'pix')]
    psum x11 -> x0, blocking collectives: 801 us -> none  [the longest x2 327 us: per_device(): top_sum = lax.psum(norm_local, 'pix')]
    pallas_call x0 -> x1, Pallas kernels: none -> 169 us  [factors(): pl.pallas_call(factor_kernel, out_shape=(jax.ShapeDtypeStruct((256, 256),...]
    dot_general x9 -> x0, matrix products: 56.5 us -> none  [the longest x2 18.1 us: per_device(): lax.dot_general(misfit, pix_fac, (((0,), (0,)), ((), ())), precision=high...]
  transfers between devices with their start and end apart: 8 -> 4, of which waited for: 7 -> 3; matrix products, arithmetic and copies ran while one was open for 0% -> 2% of each run, Pallas kernels for 0% -> 0%
where the time goes in v1:
time: 304 us; the launch traced here: 303 us
  Pallas kernels  169 us (56%)
  waiting for transfers between devices  103 us (34%)
  starting transfers between devices  14.9 us (5%)
  other arithmetic  8.39 us (3%)
  local copies, waits for them, and re-layouts  7.3 us (2%)
    pallas_call x1, Pallas kernels, factors(): pl.pallas_call(factor_kernel, out_shape=(jax.ShapeDtypeStruct((256, 256),...  169 us
    ppermute x4, waiting for transfers between devices, passed_along(): return lax.ppermute(block, axis, route)  103 us
    ppermute x4, starting transfers between devices, passed_along(): return lax.ppermute(block, axis, route)  14.9 us
    add x2, other arithmetic, smooth_pass(): return grid + diffusion * summed  8.39 us
  transfers between devices with their start and end apart: 4, of which 3 were waited for; matrix products, arithmetic and copies ran while one was open for 2% of the time, Pallas kernels for 0%

profile of v1, /device:TPU:1, one launch (start us, length us, event | category | flops | bytes accessed | tf_op | source)
XLA Modules:
  0.0 303.2 jit_solution(898943508179685217)
XLA Ops:
  0.6 168.9 %factors.1 = (f32[256,256]{1,0:T(8,128)}, f32[2048,256]{1,0:T(8,128)}, f32[256,2048]{1,0:T(8,128)}, f32[8,128]{1,0:T(8,128)}) custom-call(f32[256,2048]{1,0:T(8,128)} %obs_in.1, s32[256,256]{1,0:T(8,128)} %mask_in.1, f32[256,256]{1,0:T(8,128)} %u_in.1, f32[2048,256]{1,0:T(8,128)} %v_in.1), custom_call_target="tpu_custom_call" | custom-call | tf_op jit(solution)/shard_map/factors/pallas_call | solution.py:398
  169.5 3.1 %collective-permute-start.1 = (f32[256,2048]{1,0:T(8,128)}, f32[256,2048]{1,0:T(8,128)S(1)}, u32[]{:S(2)}, u32[]{:S(2)}) collective-permute-start(f32[256,2048]{1,0:T(8,128)} %get-tuple-element.9), channel_id=1, source_target_pairs={{2,0},{4,2},{6,4},{8,6},{10,8},{12,10},{14,12},{16,14},{18,16},{20... | collective-permute-start | bytes 6291464 | tf_op jit(solution)/shard_map/ppermute | solution.py:444
  172.6 4.0 %collective-permute-start = (f32[256,2048]{1,0:T(8,128)}, f32[256,2048]{1,0:T(8,128)}, u32[]{:S(2)}, u32[]{:S(2)}) collective-permute-start(f32[256,2048]{1,0:T(8,128)} %get-tuple-element.9), channel_id=1, source_target_pairs={{0,2},{2,4},{4,6},{6,8},{8,10},{10,12},{12,14},{14,16},{16,18},{18... | collective-permute-start | bytes 6291464 | tf_op jit(solution)/shard_map/ppermute | solution.py:444
  176.6 1.2 slice.27
  177.8 0.9 slice_bitcast_fusion.7
  178.7 0.0 copy-start
  178.7 2.7 slice_bitcast_fusion.3
  181.4 36.9 %collective-permute-done.1 = f32[256,2048]{1,0:T(8,128)S(1)} collective-permute-done((f32[256,2048]{1,0:T(8,128)}, f32[256,2048]{1,0:T(8,128)S(1)}, u32[]{:S(2)}, u32[]{:S(2)}) %collective-permute-start.1) | collective-permute-done | bytes 2097184 | tf_op jit(solution)/shard_map/ppermute | solution.py:444
  218.3 24.1 %collective-permute-done = f32[256,2048]{1,0:T(8,128)} collective-permute-done((f32[256,2048]{1,0:T(8,128)}, f32[256,2048]{1,0:T(8,128)}, u32[]{:S(2)}, u32[]{:S(2)}) %collective-permute-start) | collective-permute-done | bytes 2097184 | tf_op jit(solution)/shard_map/ppermute | solution.py:444
  242.4 0.0 copy-done
  242.4 4.2 %multiply_add_fusion.1 = f32[256,2048]{1,0:T(8,128)S(1)} fusion(f32[256,2048]{1,0:T(8,128)S(1)} %copy-done, f32[1,2048]{1,0:T(1,128)S(1)} %get-tuple-element.16, f32[255,2048]{1,0:T(8,128)S(1)} %get-tuple-element.18, f32[255,2048]{1,0:T(8,128)S(1)} %get-tuple-element.17, f32[1,2048]{1,0:T(1,128)S(1)} %get-tuple-element.15, ...), kind=kLoop, calls=%fused_computation.13 | loop fusion | flops 15204352 | bytes 12582918 | tf_op jit(solution)/shard_map/add | solution.py:466
  246.7 1.9 collective-permute-start.3
  248.6 5.9 %collective-permute-start.2 = (f32[256,2048]{1,0:T(8,128)S(1)}, f32[256,2048]{1,0:T(8,128)S(1)}, u32[]{:S(2)}, u32[]{:S(2)}) collective-permute-start(f32[256,2048]{1,0:T(8,128)S(1)} %multiply_add_fusion.1), channel_id=1, source_target_pairs={{0,2},{2,4},{4,6},{6,8},{8,10},{10,12},{12,14},{14,16},{16,18},{18... | collective-permute-start | bytes 6291464 | tf_op jit(solution)/shard_map/ppermute | solution.py:444
  254.5 0.5 slice_bitcast_fusion.1
  255.0 42.0 %collective-permute-done.3 = f32[256,2048]{1,0:T(8,128)S(1)} collective-permute-done((f32[256,2048]{1,0:T(8,128)S(1)}, f32[256,2048]{1,0:T(8,128)S(1)}, u32[]{:S(2)}, u32[]{:S(2)}) %collective-permute-start.3) | collective-permute-done | bytes 2097184 | tf_op jit(solution)/shard_map/ppermute | solution.py:444
  297.0 0.0 collective-permute-done.2
  297.0 0.0 copy-start.2
  297.0 0.0 copy-start.1
  297.0 4.1 %multiply_add_fusion = f32[256,2048]{1,0:T(8,128)} fusion(f32[256,2048]{1,0:T(8,128)S(1)} %multiply_add_fusion.1, f32[1,2048]{1,0:T(1,128)S(1)} %get-tuple-element.12, f32[255,2048]{1,0:T(8,128)S(1)} %get-tuple-element.14, f32[255,2048]{1,0:T(8,128)S(1)} %get-tuple-element.13, f32[1,2048]{1,0:T(1,128)S(1)} %get-tuple-element.11, ...), kind=kLoop, calls=%fused_computation.12 | loop fusion | flops 15204352 | bytes 12582918 | tf_op jit(solution)/shard_map/add | solution.py:466
  301.2 0.0 copy-done.2
  301.2 0.7 copy.9
  301.9 0.0 copy-done.1
  301.9 1.3 copy.10
  (1 shorter events, 0.0 us)
Async XLA Ops:
  169.5 48.8 %collective-permute-start.1 = (f32[256,2048]{1,0:T(8,128)}, f32[256,2048]{1,0:T(8,128)S(1)}, u32[]{:S(2)}, u32[]{:S(2)}) collective-permute-start(f32[256,2048]{1,0:T(8,128)} %get-tuple-element.9), channel_id=1, source_target_pairs={{2,0},{4,2},{6,4},{8,6},{10,8},{12,10},{14,12},{16,14},{18,16},{20... | collective-permute-start | bytes 6291464 | tf_op jit(solution)/shard_map/ppermute | solution.py:444
  172.6 69.8 %collective-permute-start = (f32[256,2048]{1,0:T(8,128)}, f32[256,2048]{1,0:T(8,128)}, u32[]{:S(2)}, u32[]{:S(2)}) collective-permute-start(f32[256,2048]{1,0:T(8,128)} %get-tuple-element.9), channel_id=1, source_target_pairs={{0,2},{2,4},{4,6},{6,8},{8,10},{10,12},{12,14},{14,16},{16,18},{18... | collective-permute-start | bytes 6291464 | tf_op jit(solution)/shard_map/ppermute | solution.py:444
  178.7 63.7 %copy-start = (f32[256,2048]{1,0:T(8,128)S(1)}, f32[256,2048]{1,0:T(8,128)}, u32[]{:S(2)}) copy-start(f32[256,2048]{1,0:T(8,128)} %get-tuple-element.9) | copy-start | bytes 6291460
  246.7 50.3 %collective-permute-start.3 = (f32[256,2048]{1,0:T(8,128)S(1)}, f32[256,2048]{1,0:T(8,128)S(1)}, u32[]{:S(2)}, u32[]{:S(2)}) collective-permute-start(f32[256,2048]{1,0:T(8,128)S(1)} %multiply_add_fusion.1), channel_id=1, source_target_pairs={{2,0},{4,2},{6,4},{8,6},{10,8},{12,10},{14,12},{16,14},{18,16},{20... | collective-permute-start | bytes 6291464 | tf_op jit(solution)/shard_map/ppermute | solution.py:444
  248.6 48.4 %collective-permute-start.2 = (f32[256,2048]{1,0:T(8,128)S(1)}, f32[256,2048]{1,0:T(8,128)S(1)}, u32[]{:S(2)}, u32[]{:S(2)}) collective-permute-start(f32[256,2048]{1,0:T(8,128)S(1)} %multiply_add_fusion.1), channel_id=1, source_target_pairs={{0,2},{2,4},{4,6},{6,8},{8,10},{10,12},{12,14},{14,16},{16,18},{18... | collective-permute-start | bytes 6291464 | tf_op jit(solution)/shard_map/ppermute | solution.py:444
  297.0 4.1 %copy-start.2 = (f32[256,256]{1,0:T(8,128)S(1)}, f32[256,256]{1,0:T(8,128)}, u32[]{:S(2)}) copy-start(f32[256,256]{1,0:T(8,128)} %get-tuple-element.22) | copy-start | bytes 786436
  297.0 4.8 %copy-start.1 = (f32[2048,256]{1,0:T(8,128)S(1)}, f32[2048,256]{1,0:T(8,128)}, u32[]{:S(2)}) copy-start(f32[2048,256]{1,0:T(8,128)} %get-tuple-element.23) | copy-start | bytes 6291460

commit v2 on v1

v2 whole, which is shorter than its diff:
```python
import jax
import jax.numpy as jnp
from jax import lax
from jax.experimental import pallas as pl
from jax.experimental.pallas import tpu as pltpu
from jax.sharding import PartitionSpec as P

BANDS = 8
WIDTH = 256
ITERS = 2
TILE = 256
TILES = 8
CHUNKS = 16
TOTAL = 67108864.0
diffusion = 0.2

f32 = jnp.float32
bf16 = jnp.bfloat16
MESH = pl.DeviceIdType.MESH


def split(x):
    hi = x.astype(bf16)
    return hi, (x - hi.astype(f32)).astype(bf16)


def mm(a, b):
    return lax.dot_general(a, b, (((1,), (0,)), ((), ())), preferred_element_type=f32)


def mm_nt(a, b):
    return lax.dot_general(a, b, (((1,), (1,)), ((), ())), preferred_element_type=f32)


def fold(x):
    part = x.reshape(x.shape[0] // 8, 8, x.shape[1]).sum(axis=0)
    return part[:, :128] + part[:, 128:]


def pack(*parts):
    rows = [jnp.sum(part, axis=0, keepdims=True) for part in parts]
    rows.append(jnp.zeros((8 - len(rows), 128), f32))
    return jnp.concatenate(rows, axis=0)


def kernel(
    obs_in, mask_in, u_in, v_in,
    u_out, v_out, cloud_out,
    r, w, c, vt, vs, hp, hsib, hf, vio, lay, mask, spread,
    u, us, uts, gp, gr, gs, n1, n2, s1, s2, lev,
    hx, mh, uh, uhs, ya, yb, fb,
    in_sem, out_sem, ss1, rs1, ss2, rs2, gss, grs, sibs, sibr,
    r1s, r1r, r2s, r2r, a2s, a2r, a1s, a1r, fs, fr,
    hys, hyr, hzs, hzr, h1s, h1r, h2s, h2r,
):
    p = lax.axis_index("pix")
    lo = lax.axis_index("col")
    core, h, z, x = p % 2, (p // 2) % 2, (p // 4) % 4, p // 16

    def dev(x, z, h, core, lo):
        return {"pix": ((x * 4 + z) * 2 + h) * 2 + core, "col": lo}

    i1 = (h * 2 + core) * 2 + lo
    i2 = x * 4 + z

    def peer1(d):
        j = (i1 + d) % 8
        return dev(x, z, j // 4, (j // 2) % 2, j % 2)

    def peer2(d):
        j = (i2 + d) % 16
        return dev(j // 4, j % 4, h, core, lo)

    sibling = dev(x, z, h, 1 - core, lo)
    col_pair = dev(x, z, h, core, 1 - lo)
    y_pair = dev(x, z, 1 - h, core, lo)
    z_next = peer2(17 - 2 * h)
    q1 = x + core * (z - x)
    q2 = z + core * (x - z)
    iy = 2 + (h + core) % 2
    iz = 5 - iy

    def ring1(q):
        return dev(q + core * (x - q), z + core * (q - z), h, core, lo)

    def ring2(q, h):
        return dev(x + core * (q - x), q + core * (z - q), h, core, lo)

    def rcopy(src, dst, send, recv, to):
        return pltpu.make_async_remote_copy(
            src_ref=src, dst_ref=dst, send_sem=send, recv_sem=recv, device_id=to, device_id_type=MESH
        )

    def each(low, high, step):
        def body(i, _):
            step(i)
            return 0

        lax.fori_loop(low, high, body, 0)

    barrier = pltpu.get_barrier_semaphore()
    for d in range(1, 8):
        pl.semaphore_signal(barrier, inc=1, device_id=peer1(d), device_id_type=MESH)
    for d in range(1, 16):
        pl.semaphore_signal(barrier, inc=1, device_id=peer2(d), device_id_type=MESH)

    loads = [pltpu.make_async_copy(v_in.at[pl.ds(t * TILE, TILE)], vio.at[t], in_sem.at[t]) for t in range(TILES)]
    loads.append(pltpu.make_async_copy(u_in, u, in_sem.at[TILES]))
    loads.append(pltpu.make_async_copy(mask_in, mask, in_sem.at[TILES + 1]))
    for t in range(TILES):
        loads.append(
            pltpu.make_async_copy(obs_in.at[:, pl.ds(t * TILE, TILE)], r.at[t], in_sem.at[TILES + 2 + t])
        )
    for load in loads:
        load.start()
    for part in range(4):
        date = lax.broadcasted_iota(jnp.int32, (128, TILE), 0)
        column = lax.broadcasted_iota(jnp.int32, (128, TILE), 1) + part * TILE
        gap = column - date * BANDS
        spread[part] = jnp.where((gap >= 0) & (gap < BANDS), 1.0, 0.0).astype(bf16)

    MASK, PIX = CHUNKS, CHUNKS + 1

    def chunk(i):
        return i // 2, pl.ds(pl.multiple_of((i % 2) * 128, 128), 128)

    def y_obs(i, slot):
        t, rows = chunk(i)
        cols = pl.ds(pl.multiple_of(t * TILE, TILE), TILE)
        return rcopy(obs_in.at[rows, cols], hx.at[slot, t, rows], hys.at[i], hyr.at[i], y_pair)

    def z_obs(i):
        t, rows = chunk(i)
        return rcopy(hx.at[iy, t, rows], hx.at[iz, t, rows], hzs.at[i], hzr.at[i], z_next)

    def y_send(i):
        y_obs(i, iz).start()

    def z_send(i):
        y_obs(i, iy).wait_recv()
        z_obs(i).start()

    def y_mask(slot):
        return rcopy(mask_in, mh.at[slot], hys.at[MASK], hyr.at[MASK], y_pair)

    def y_pix(slot):
        return rcopy(u, uh.at[slot], hys.at[PIX], hyr.at[PIX], y_pair)

    z_mask = rcopy(mh.at[iy], mh.at[iz], hzs.at[MASK], hzr.at[MASK], z_next)
    z_pix = rcopy(uh.at[iy], uh.at[iz], hzs.at[PIX], hzr.at[PIX], z_next)
    s1_mask = rcopy(mask_in, mh.at[0], h1s.at[TILES], h1r.at[TILES], sibling)
    s1_pix = rcopy(u, uh.at[0], h1s.at[TILES + 1], h1r.at[TILES + 1], sibling)

    def s1_obs(t):
        cols = pl.ds(pl.multiple_of(t * TILE, TILE), TILE)
        return rcopy(obs_in.at[:, cols], hx.at[0, t], h1s.at[t], h1r.at[t], sibling)

    def s2_obs(t):
        return rcopy(hx.at[2, t], hx.at[1, t], h2s.at[t], h2r.at[t], sibling)

    s2_mask = rcopy(mh.at[2], mh.at[1], h2s.at[TILES], h2r.at[TILES], sibling)
    s2_pix = rcopy(uh.at[2], uh.at[1], h2s.at[TILES + 1], h2r.at[TILES + 1], sibling)

    pl.semaphore_wait(barrier, 22)
    y_mask(iz).start()
    y_send(0)
    s1_mask.start()
    each(0, TILES, lambda t: s1_obs(t).start())

    for load in loads[: TILES]:
        load.wait()

    def turn_v(t):
        vt_t = jnp.transpose(vio[t])
        vt[t] = vt_t
        hi, low = split(vt_t)
        vs[t, 0] = hi
        vs[t, 1] = low

    each(0, TILES, turn_v)
    for load in loads[TILES:]:
        load.wait()

    def set_u(value):
        u[...] = value
        hi, low = split(value)
        us[0] = hi
        us[1] = low

    set_u(u[...])

    def dot3(a_ref, hi, low):
        return mm(a_ref[0], hi) + mm(a_ref[0], low) + mm(a_ref[1], hi)

    def weight(mask_ref, t):
        dates = mask_ref[:, pl.ds(pl.multiple_of((t // 4) * 128, 128), 128)].astype(f32).astype(bf16)
        return mm(dates, spread[t % 4])

    def first(t, acc):
        w_t = weight(mask, t)
        w[t] = w_t
        r_t = w_t * (r[t] - dot3(us, vs[t, 0], vs[t, 1]))
        r[t] = r_t
        return acc + fold(r_t * r_t)

    zero = jnp.zeros((8, 128), f32)
    square = lax.fori_loop(0, TILES, first, zero)

    def all_reduce(k, message, between):
        s1[k, i1] = message
        for d in range(1, 8):
            rcopy(s1.at[k, i1], s1.at[k, i1], ss1.at[k], rs1.at[k], peer1(d)).start()
        whole = s1.at[k, pl.ds(0, 7)]
        done1 = rcopy(whole, whole, ss1.at[k], rs1.at[k], sibling)
        done1.wait_recv()
        total = s1[k, 0]
        for j in range(1, 8):
            total = total + s1[k, j]
        s2[k, i2] = total
        for d in range(1, 16):
            rcopy(s2.at[k, i2], s2.at[k, i2], ss2.at[k], rs2.at[k], peer2(d)).start()
        between()
        whole = s2.at[k, pl.ds(0, 15)]
        done2 = rcopy(whole, whole, ss2.at[k], rs2.at[k], ring1((q1 + 1) % 4))
        done2.wait_recv()
        total = s2[k, 0]
        for j in range(1, 16):
            total = total + s2[k, j]
        done1.wait_send()
        done2.wait_send()
        return jnp.sum(total, axis=1, keepdims=True)

    def level_from(square):
        return jnp.sqrt(jnp.maximum(square, 0.0) / TOTAL + 1e-06)

    sums = all_reduce(0, pack(square), lambda: each(1, 3, y_send))
    lev[...] = jnp.broadcast_to(level_from(sums[0:1]), (8, 128))
    y_mask(iy).wait_recv()
    z_mask.start()

    def cut(value, level):
        return jnp.minimum(jnp.maximum(value, -level), level)

    mine, other = 4 * core, 4 * (1 - core)

    def y_more(low, high):
        each(jnp.minimum(low, CHUNKS), jnp.minimum(high, CHUNKS), y_send)

    def iteration(it, _):
        level = lev[0:1, 0:1]
        y0, z0 = 3 + 10 * it, 4 * it

        each(z0, z0 + 2 * it, z_send)
        copies = []
        for part in range(2):
            rows = pl.ds(part * 128, 128)

            def grow(t, acc):
                hi, low = split(cut(r[t, rows, :], level))
                v_hi, v_low = vs[t, 0], vs[t, 1]
                return acc + mm_nt(hi, v_hi) + mm_nt(hi, v_low) + mm_nt(low, v_hi)

            gp[rows, :] = lax.fori_loop(0, TILES, grow, jnp.zeros((128, TILE), f32))
            copies.append(rcopy(gp.at[rows], gr.at[rows], gss.at[part], grs.at[part], col_pair))
            copies[-1].start()
        z1 = z0 + 2 * it
        each(z1, z1 + 2 + it, z_send)
        z2 = z1 + 2 + it
        for copy in copies:
            copy.wait()
        g = gp[...] + gr[...]
        gp[...] = g
        hi, low = split(g)
        gs[0] = hi
        gs[1] = low

        def curve(t, acc):
            c_t = w[t] * dot3(gs, vs[t, 0], vs[t, 1])
            c[t] = c_t
            return acc + fold(c_t * c_t)

        bottom = lax.fori_loop(0, TILES, curve, zero)
        z_send(z2)
        sums = all_reduce(1 + 2 * it, pack(fold(g * g) * 0.5, bottom), lambda: y_more(y0, y0 + 1))
        step = sums[0:1] / sums[1:2]
        set_u(u[...] + step * gp[...])
        hi, low = split(jnp.transpose(u[...]))
        uts[0] = hi
        uts[1] = low

        @pl.when(it == ITERS - 1)
        def _():
            y_pix(iz).start()
            s1_pix.start()

        y_more(y0 + 1, y0 + 5)

        def pull(t):
            r_t, ac = r[t], step * c[t]
            r[t] = r_t - ac
            hi, low = split(cut(r_t, level) - ac)
            hp[t] = dot3(uts, hi, low)

        def order(i):
            return jnp.where(i == 0, 2, jnp.where(i == 1, 1, jnp.where(i == 2, 3, 0)))

        def hand(k, slot):
            return rcopy(hp.at[other + k], hsib.at[slot], sibs.at[slot], sibr.at[slot], sibling)

        def reduce1(d):
            return rcopy(hp.at[mine + (q1 + d) % 4], n1.at[d - 1], r1s.at[d - 1], r1r.at[d - 1], ring1((q1 + d) % 4))

        def pull_step(i):
            @pl.when(i < 4)
            def _():
                d = order(i)
                pull(other + (q2 + d) % 4)
                hand((q2 + d) % 4, d).start()
                pull(mine + (q1 + d) % 4)

            @pl.when(i >= 2)
            def _():
                d = order(i - 2)
                hand(0, d).wait_recv()
                tile = mine + (q1 + d) % 4
                hp[tile] = hp[tile] + hsib[d]

                @pl.when(i < 5)
                def _():
                    reduce1(d).start()

        each(0, 6, pull_step)
        for d in (1, 3, 2):
            reduce1(d).wait_recv()
        tile = mine + q1
        hp[tile] = hp[tile] + n1[0] + n1[1] + n1[2]

        j2 = q2 * 2 + h

        def sub(ref, j):
            return ref.at[tile, pl.ds(pl.multiple_of(32 * j, 32), 32)]

        def reduce2(e):
            j = (j2 + e) % 8
            return rcopy(sub(hp, j), n2.at[e - 1], r2s.at[e - 1], r2r.at[e - 1], ring2(j // 2, j % 2))

        for e in range(1, 8):
            reduce2(e).start()

        @pl.when(it == ITERS - 1)
        def _():
            y_pix(iy).wait_recv()
            z_pix.start()

        for e in range(1, 8):
            reduce2(e).wait_recv()
        piece = sub(hp, j2)[...]
        for e in range(7):
            piece = piece + n2[e]
        sub(hf, j2)[...] = piece
        norm = fold(piece * piece)

        def gather2(e, j):
            to = (j2 + e) % 8
            return rcopy(sub(hf, j), sub(hf, j), a2s.at[e - 1], a2r.at[e - 1], ring2(to // 2, to % 2))

        for e in range(1, 8):
            gather2(e, j2).start()
        for e in range(1, 8):
            gather2(e, (j2 + 8 - e) % 8).wait_recv()

        def gather1(d, k):
            return rcopy(hf.at[mine + k], hf.at[mine + k], a1s.at[d - 1], a1r.at[d - 1], ring1((q1 + d) % 4))

        for d in (2, 1, 3):
            gather1(d, q1).start()
        y_more(y0 + 5, y0 + 9)

        def shift(t, accs):
            hi, low = split(hf[t])
            s_t = w[t] * dot3(us, hi, low)
            c[t] = s_t
            r_t = r[t]
            a0, a1, a2 = accs
            return a0 + fold(r_t * r_t), a1 + fold(r_t * s_t), a2 + fold(s_t * s_t)

        def pass_on(k, i, half):
            return rcopy(hf.at[half + k], hf.at[half + k], fs.at[i], fr.at[i], sibling)

        def shift_step(i, accs):
            d = jnp.where(i == 2, 3, jnp.where(i == 3, 2, i))
            k = (q1 + 4 - d) % 4

            @pl.when(i > 0)
            def _():
                gather1(d, k).wait_recv()

            pass_on(k, i, mine).start()
            accs = shift(mine + k, accs)
            k = (q2 + 4 - d) % 4
            pass_on(k, i, other).wait_recv()
            return shift(other + k, accs)

        accs = lax.fori_loop(0, 4, shift_step, (zero, zero, zero))
        for d in (1, 2, 3):
            reduce1(d).wait_send()
            gather1(d, q1).wait_send()
        for e in range(1, 8):
            reduce2(e).wait_send()
            gather2(e, j2).wait_send()
        for i in range(4):
            hand(i, i).wait_send()
            pass_on(i, i, mine).wait_send()
        z_send(z2 + 1)
        sums = all_reduce(2 + 2 * it, pack(norm, *accs), lambda: y_more(y0 + 9, y0 + 10))
        step = sums[0:1] / sums[3:4]
        square = sums[1:2] - 2.0 * step * sums[2:3] + step * step * sums[3:4]
        lev[...] = jnp.broadcast_to(level_from(square), (8, 128))

        @pl.when(it == ITERS - 1)
        def _():
            each(z2 + 2, CHUNKS, z_send)

        def update(t):
            v_t = vt[t] + step * hf[t]
            vt[t] = v_t
            hi, low = split(v_t)
            vs[t, 0] = hi
            vs[t, 1] = low
            r[t] = r[t] - step * c[t]

        each(0, TILES, update)
        return 0

    lax.fori_loop(0, ITERS, iteration, 0)
    stores = [pltpu.make_async_copy(u, u_out, out_sem.at[0])]
    stores[0].start()

    z_mask.wait_recv()
    s2_mask.start()
    z_pix.wait_recv()
    s2_pix.start()
    s1_mask.wait_recv()
    s1_pix.wait_recv()
    s2_mask.wait_recv()
    s2_pix.wait_recv()
    for k in range(4):
        hi, low = split(uh[k])
        uhs[k, 0] = hi
        uhs[k, 1] = low
    level = lev[0:1, 0:1]
    inverse = 1.0 / level
    last = 63
    side = 1 - 2 * core

    def flag(offset):
        row = p + offset
        return ((row >= 0) & (row <= last)).astype(f32)

    has1, has2, has3 = flag(-side), flag(2 * side), flag(-2 * side)

    def soft(scaled):
        return scaled - jnp.minimum(jnp.maximum(scaled, -1.0), 1.0)

    def g(e):
        return e / (1.0 + e * e)

    def ready(t):
        z_obs(2 * t).wait_recv()
        z_obs(2 * t + 1).wait_recv()
        s2_obs(t).start()

    STRIP = 32
    AT = 8

    def rim(ref):
        ref[AT - 1 : AT, :] = ref[AT : AT + 1, :]
        ref[AT + WIDTH : AT + WIDTH + 1, :] = ref[AT + WIDTH - 1 : AT + WIDTH, :]

    def along(src, dst):
        def strip(i):
            at = pl.multiple_of(i * STRIP, STRIP)
            block = src[pl.ds(at + AT, STRIP + 8), :]
            dst[pl.ds(at + AT, STRIP), :] = g(block[1 : STRIP + 1] - block[:STRIP])

        each(0, WIDTH // STRIP, strip)

    def smooth_tile(t):
        @pl.when(t + 1 < TILES)
        def _():
            ready(t + 1)

        s1_obs(t).wait_recv()
        s2_obs(t).wait_recv()
        ya[4, AT : AT + WIDTH, :] = soft(r[t] * inverse)

        def halo(k):
            r_k = hx[k, t] - dot3(uhs.at[k], vs[t, 0], vs[t, 1])
            ya[k, AT : AT + WIDTH, :] = weight(mh.at[k], t) * soft(r_k * inverse)

        each(0, 4, halo)
        for k in (0, 1, 4):
            rim(ya.at[k])
        for row, k in ((0, 0), (1, 1), (2, 4)):
            along(ya.at[k], fb.at[row])

        def net(row, at):
            block = fb[row, pl.ds(at, STRIP + 8), :]
            return block[8:] - block[7 : STRIP + 7]

        def pass1(i):
            at = pl.multiple_of(i * STRIP, STRIP)
            rows = pl.ds(at + AT, STRIP)
            y0, y1, y2, y3, own = [ya[k, rows, :] for k in range(5)]
            to0 = g(y0 - own)
            to1 = g(has1 * (y1 - own))
            yb[2, rows, :] = own + diffusion * (to0 + to1 + net(2, at))
            yb[0, rows, :] = y0 + diffusion * (g(has2 * (y2 - y0)) - to0 + net(0, at))
            yb[1, rows, :] = y1 + diffusion * (g(has3 * (y3 - y1)) - to1 + net(1, at))

        each(0, WIDTH // STRIP, pass1)
        rim(yb.at[2])
        along(yb.at[2], fb.at[2])

        def pass2(i):
            at = pl.multiple_of(i * STRIP, STRIP)
            rows = pl.ds(at + AT, STRIP)
            own = yb[2, rows, :]
            total = g(yb[0, rows, :] - own) + g(has1 * (yb[1, rows, :] - own)) + net(2, at)
            lay[t, pl.ds(at, STRIP), :] = level * (own + diffusion * total)

        each(0, WIDTH // STRIP, pass2)
        cloud_store(t).start()
        vio[t] = jnp.transpose(vt[t])
        v_store(t).start()

    def cloud_store(t):
        cols = pl.ds(pl.multiple_of(t * TILE, TILE), TILE)
        return pltpu.make_async_copy(lay.at[t], cloud_out.at[:, cols], out_sem.at[1 + t])

    def v_store(t):
        rows = pl.ds(pl.multiple_of(t * TILE, TILE), TILE)
        return pltpu.make_async_copy(vio.at[t], v_out.at[rows], out_sem.at[1 + TILES + t])

    for row in range(3):
        fb[row, :AT, :] = jnp.zeros((AT, TILE), f32)
    ready(0)
    each(0, TILES, smooth_tile)
    stores[0].wait()
    y_mask(iz).wait_send()
    y_pix(iz).wait_send()
    for copy in (z_mask, z_pix, s1_mask, s1_pix, s2_mask, s2_pix):
        copy.wait_send()

    def drain(i):
        y_obs(i, iz).wait_send()
        z_obs(i).wait_send()

    each(0, CHUNKS, drain)

    def close(t):
        s1_obs(t).wait_send()
        s2_obs(t).wait_send()
        cloud_store(t).wait()
        v_store(t).wait()

    each(0, TILES, close)


def per_device(observed, valid_mask, pix_factor, col_factor):
    any_space = pl.BlockSpec(memory_space=pl.ANY)
    full = pltpu.VMEM((TILES, TILE, TILE), f32)
    square = pltpu.VMEM((TILE, TILE), f32)
    pair = pltpu.VMEM((2, TILE, TILE), bf16)
    dma = pltpu.SemaphoreType.DMA
    return pl.pallas_call(
        kernel,
        out_shape=(
            jax.ShapeDtypeStruct((256, 256), f32),
            jax.ShapeDtypeStruct((2048, 256), f32),
            jax.ShapeDtypeStruct((256, 2048), f32),
        ),
        in_specs=[any_space] * 4,
        out_specs=[any_space] * 3,
        scratch_shapes=[
            full, full, full, full,
            pltpu.VMEM((TILES, 2, TILE, TILE), bf16),
            full,
            pltpu.VMEM((4, TILE, TILE), f32),
            full, full, full,
            pltpu.VMEM((256, 256), jnp.int32),
            pltpu.VMEM((4, 128, TILE), bf16),
            square, pair, pair, square, square, pair,
            pltpu.VMEM((3, TILE, TILE), f32),
            pltpu.VMEM((7, 32, TILE), f32),
            pltpu.VMEM((5, 8, 8, 128), f32),
            pltpu.VMEM((5, 16, 8, 128), f32),
            pltpu.VMEM((8, 128), f32),
            pltpu.VMEM((4, TILES, TILE, TILE), f32),
            pltpu.VMEM((4, 256, 256), jnp.int32),
            pltpu.VMEM((4, TILE, TILE), f32),
            pltpu.VMEM((4, 2, TILE, TILE), bf16),
            pltpu.VMEM((5, TILE + 16, TILE), f32),
            pltpu.VMEM((3, TILE + 16, TILE), f32),
            pltpu.VMEM((3, TILE + 16, TILE), f32),
            dma((2 * TILES + 2,)), dma((2 * TILES + 1,)),
            dma((5,)), dma((5,)), dma((5,)), dma((5,)),
            dma((2,)), dma((2,)), dma((4,)), dma((4,)),
            dma((3,)), dma((3,)), dma((7,)), dma((7,)),
            dma((7,)), dma((7,)), dma((3,)), dma((3,)), dma((4,)), dma((4,)),
            dma((CHUNKS + 2,)), dma((CHUNKS + 2,)), dma((CHUNKS + 2,)), dma((CHUNKS + 2,)),
            dma((TILES + 2,)), dma((TILES + 2,)), dma((TILES + 2,)), dma((TILES + 2,)),
        ],
        compiler_params=pltpu.CompilerParams(
            collective_id=0, has_side_effects=True, vmem_limit_bytes=60 * 1024 * 1024
        ),
        name="separate",
    )(observed, valid_mask, pix_factor, col_factor)


def solution(mesh):
    in_specs = (P("pix", "col"), P("pix", "col"), P("pix", None), P("col", None))
    out_specs = (P("pix", None), P("col", None), P("pix", "col"))
    return jax.shard_map(
        per_device, mesh=mesh, in_specs=in_specs, out_specs=out_specs, check_vma=False
    )
```

time: 304 us -> 197 us (0.65)
  waiting for transfers between devices: 103 us -> 0 us
  Pallas kernels: 169 us -> 190 us
  starting transfers between devices: 14.9 us -> 0 us
  other arithmetic: 8.39 us -> 0 us
    ppermute x4 -> x0, waiting for transfers between devices: 103 us -> none  [passed_along(): return lax.ppermute(block, axis, route)]
    pallas_call x1, Pallas kernels: 169 us -> 190 us  [per_device(): pl.pallas_call(kernel, out_shape=(jax.ShapeDtypeStruct((256, 256), f32),...]
    ppermute x4 -> x0, starting transfers between devices: 14.9 us -> none  [passed_along(): return lax.ppermute(block, axis, route)]
    add x2 -> x0, other arithmetic: 8.39 us -> none  [smooth_pass(): return grid + diffusion * summed]
    unnamed x8 -> x5, local copies, waits for them, and re-layouts: 2.03 us -> 6.19 us
    concatenate x4 -> x0, local copies, waits for them, and re-layouts: 4.08 us -> none  [smooth_pass(): west = jnp.concatenate([grid[:, :1], grid[:, :-1]], axis=1)]
  transfers between devices with their start and end apart: 4 -> 0, of which waited for: 3 -> 0; matrix products, arithmetic and copies ran while one was open for 2% -> 0% of each run, Pallas kernels for 0% -> 0%
where the time goes in v2:
time: 197 us
  Pallas kernels  190 us (96%)
  local copies, waits for them, and re-layouts  6.19 us (3%)
    pallas_call x1, Pallas kernels, per_device(): pl.pallas_call(kernel, out_shape=(jax.ShapeDtypeStruct((256, 256), f32),...  190 us
    unnamed x5, local copies, waits for them, and re-layouts  6.19 us

profile of v2, /device:TPU:1, one launch (start us, length us, event | category | flops | bytes accessed | tf_op | source)
XLA Modules:
  0.0 197.0 jit_solution(7075479369645204574)
XLA Ops:
  0.6 190.2 %separate.1 = (f32[256,256]{1,0:T(8,128)}, f32[2048,256]{1,0:T(8,128)}, f32[256,2048]{1,0:T(8,128)}) custom-call(f32[256,2048]{1,0:T(8,128)} %obs_in.1, s32[256,256]{1,0:T(8,128)} %mask_in.1, f32[256,256]{1,0:T(8,128)} %u_in.1, f32[2048,256]{1,0:T(8,128)} %v_in.1), custom_call_target="tpu_custom_call" | custom-call | tf_op jit(solution)/shard_map/separate/pallas_call | solution.py:576
  190.8 1.7 copy.10
  192.5 0.0 copy-start
  192.5 3.2 %copy.11 = f32[2048,256]{1,0:T(8,128)} copy(f32[2048,256]{1,0:T(8,128)} %get-tuple-element.7) | data formatting | bytes 4194304
  195.7 0.0 copy-done
  195.7 1.3 copy.12
Async XLA Ops:
  192.5 3.2 %copy-start = (f32[256,2048]{1,0:T(8,128)S(1)}, f32[256,2048]{1,0:T(8,128)}, u32[]{:S(2)}) copy-start(f32[256,2048]{1,0:T(8,128)} %get-tuple-element.8) | copy-start | bytes 6291460

commit v3 on v2

v3 whole, which is shorter than its diff:
```python
import jax
import jax.numpy as jnp
from jax import lax
from jax.experimental import pallas as pl
from jax.experimental.pallas import tpu as pltpu
from jax.sharding import PartitionSpec as P

BANDS = 8
WIDTH = 256
ITERS = 2
TILE = 256
TILES = 8
CHUNKS = 16
Z_MARKS = (6, 7, 10)
AHEAD = 13

TOTAL = 67108864.0
diffusion = 0.2

f32 = jnp.float32
bf16 = jnp.bfloat16
MESH = pl.DeviceIdType.MESH


def split(x):
    hi = x.astype(bf16)
    return hi, (x - hi.astype(f32)).astype(bf16)


def left(x):
    hi, low = split(x)
    return jnp.concatenate([hi, hi, low], axis=1)


def right(x):
    hi, low = split(x)
    return jnp.concatenate([hi, low, hi], axis=0)


def mm(a, b):
    return lax.dot_general(a, b, (((1,), (0,)), ((), ())), preferred_element_type=f32)


def mm_nt(a, b):
    return lax.dot_general(a, b, (((1,), (1,)), ((), ())), preferred_element_type=f32)


def fold(x):
    part = x.reshape(x.shape[0] // 8, 8, x.shape[1]).sum(axis=0)
    return part[:, :128] + part[:, 128:]


def pack(*parts):
    rows = [jnp.sum(part, axis=0, keepdims=True) for part in parts]
    rows += [jnp.zeros((1, 128), f32)] * (4 - len(rows))
    return jnp.concatenate(rows, axis=0)


def kernel(
    obs_in, mask_in, u_in, v_in,
    u_out, v_out, cloud_out,
    r, w, c, vt, vs, hp, hsib, hf, vio, lay, mask, spread,
    u, us, uts, gp, gr, gt, gs, n1, n2, s1, s2, lev,
    hx, mh, uh, uhs, low_rank, low_shift, lev2, hw, way, ya, yb, fb,
    in_sem, out_sem, ss1, rs1, ss2, rs2, gss, grs, sibs, sibr,
    r1s, r1r, r2s, r2r, a2s, a2r, a1s, a1r, fs, fr,
    was, war, wbs, wbr, hys, hyr, hzs, hzr, h1s, h1r, h2s, h2r,
):
    p = lax.axis_index("pix")
    lo = lax.axis_index("col")
    core, h, z, x = p % 2, (p // 2) % 2, (p // 4) % 4, p // 16

    def dev(x, z, h, core, lo):
        return {"pix": ((x * 4 + z) * 2 + h) * 2 + core, "col": lo}

    i1 = (h * 2 + core) * 2 + lo
    i2 = x * 4 + z

    def peer1(d):
        j = (i1 + d) % 8
        return dev(x, z, j // 4, (j // 2) % 2, j % 2)

    def peer2(d):
        j = (i2 + d) % 16
        return dev(j // 4, j % 4, h, core, lo)

    sibling = dev(x, z, h, 1 - core, lo)
    col_pair = dev(x, z, h, core, 1 - lo)
    y_pair = dev(x, z, 1 - h, core, lo)
    z_next = peer2(17 - 2 * h)
    q1 = x + core * (z - x)
    q2 = z + core * (x - z)
    iy = 2 + (h + core) % 2
    iz = 5 - iy

    def ring1(q):
        return dev(q + core * (x - q), z + core * (q - z), h, core, lo)

    def ring2(q, h):
        return dev(x + core * (q - x), q + core * (z - q), h, core, lo)

    def rcopy(src, dst, send, recv, to):
        return pltpu.make_async_remote_copy(
            src_ref=src, dst_ref=dst, send_sem=send, recv_sem=recv, device_id=to, device_id_type=MESH
        )

    def each(low, high, step):
        def body(i, _):
            step(i)
            return 0

        lax.fori_loop(low, high, body, 0)

    barrier = pltpu.get_barrier_semaphore()
    for d in range(1, 8):
        pl.semaphore_signal(barrier, inc=1, device_id=peer1(d), device_id_type=MESH)
    for d in range(1, 16):
        pl.semaphore_signal(barrier, inc=1, device_id=peer2(d), device_id_type=MESH)

    loads = [pltpu.make_async_copy(v_in.at[pl.ds(t * TILE, TILE)], vio.at[t], in_sem.at[t]) for t in range(TILES)]
    loads.append(pltpu.make_async_copy(u_in, u, in_sem.at[TILES]))
    loads.append(pltpu.make_async_copy(mask_in, mask, in_sem.at[TILES + 1]))
    for t in range(TILES):
        loads.append(
            pltpu.make_async_copy(obs_in.at[:, pl.ds(t * TILE, TILE)], r.at[t], in_sem.at[TILES + 2 + t])
        )
    for load in loads:
        load.start()
    for part in range(4):
        date = lax.broadcasted_iota(jnp.int32, (128, TILE), 0)
        column = lax.broadcasted_iota(jnp.int32, (128, TILE), 1) + part * TILE
        gap = column - date * BANDS
        spread[part] = jnp.where((gap >= 0) & (gap < BANDS), 1.0, 0.0).astype(bf16)

    MASK, PIX = CHUNKS, CHUNKS + 1

    def chunk(i):
        return i // 2, pl.ds(pl.multiple_of((i % 2) * 128, 128), 128)

    def y_obs(i, slot):
        t, rows = chunk(i)
        cols = pl.ds(pl.multiple_of(t * TILE, TILE), TILE)
        return rcopy(obs_in.at[rows, cols], hx.at[slot, t, rows], hys.at[i], hyr.at[i], y_pair)

    def z_obs(i):
        t, rows = chunk(i)
        return rcopy(hx.at[iy, t, rows], hx.at[iz, t, rows], hzs.at[i], hzr.at[i], z_next)

    def ahead(i):
        t, rows = chunk(i)
        cols = pl.ds(pl.multiple_of(t * TILE, TILE), TILE)
        return rcopy(obs_in.at[rows, cols], way.at[i - AHEAD], was.at[i - AHEAD], war.at[i - AHEAD], peer2(15 + 2 * h))

    def across(i, slot):
        t, rows = chunk(i)
        return rcopy(way.at[i - AHEAD], hx.at[slot, t, rows], wbs.at[i - AHEAD], wbr.at[i - AHEAD], y_pair)

    def y_send(i):
        y_obs(i, iz).start()

    def z_send(i):
        y_obs(i, iy).wait_recv()
        z_obs(i).start()

    def y_mask(slot):
        return rcopy(mask_in, mh.at[slot], hys.at[MASK], hyr.at[MASK], y_pair)

    def y_pix(slot):
        return rcopy(u, uh.at[slot], hys.at[PIX], hyr.at[PIX], y_pair)

    z_mask = rcopy(mh.at[iy], mh.at[iz], hzs.at[MASK], hzr.at[MASK], z_next)
    z_pix = rcopy(uh.at[iy], uh.at[iz], hzs.at[PIX], hzr.at[PIX], z_next)
    s1_mask = rcopy(mask_in, mh.at[0], h1s.at[TILES], h1r.at[TILES], sibling)
    s1_pix = rcopy(u, uh.at[0], h1s.at[TILES + 1], h1r.at[TILES + 1], sibling)

    def s1_obs(t):
        cols = pl.ds(pl.multiple_of(t * TILE, TILE), TILE)
        return rcopy(obs_in.at[:, cols], hx.at[0, t], h1s.at[t], h1r.at[t], sibling)

    def s2_obs(t):
        return rcopy(hx.at[2, t], hx.at[1, t], h2s.at[t], h2r.at[t], sibling)

    s2_mask = rcopy(mh.at[2], mh.at[1], h2s.at[TILES], h2r.at[TILES], sibling)
    s2_pix = rcopy(uh.at[2], uh.at[1], h2s.at[TILES + 1], h2r.at[TILES + 1], sibling)

    for load in loads[: TILES]:
        load.wait()

    def turn_v(t):
        vt_t = jnp.transpose(vio[t])
        vt[t] = vt_t
        vs[t] = right(vt_t)

    each(0, TILES, turn_v)
    for load in loads[TILES:]:
        load.wait()

    def set_u(value):
        u[...] = value
        us[...] = left(value)

    set_u(u[...])

    def weight(mask_ref, t):
        dates = mask_ref[:, pl.ds(pl.multiple_of((t // 4) * 128, 128), 128)].astype(f32).astype(bf16)
        return mm(dates, spread[t % 4])

    def first(t, acc):
        w_t = weight(mask, t)
        w[t] = w_t
        r_t = w_t * (r[t] - mm(us[...], vs[t]))
        r[t] = r_t
        return acc + fold(r_t * r_t)

    zero = jnp.zeros((8, 128), f32)
    square = lax.fori_loop(0, TILES, first, zero)

    def all_reduce(k, message, between, early=lambda: None):
        s1[k, i1] = message
        for d in range(1, 8):
            rcopy(s1.at[k, i1], s1.at[k, i1], ss1.at[k], rs1.at[k], peer1(d)).start()
        whole = s1.at[k, pl.ds(0, 7)]
        done1 = rcopy(whole, whole, ss1.at[k], rs1.at[k], sibling)
        early()
        done1.wait_recv()
        total = s1[k, 0]
        for j in range(1, 8):
            total = total + s1[k, j]
        s2[k, i2] = total
        for d in range(1, 16):
            rcopy(s2.at[k, i2], s2.at[k, i2], ss2.at[k], rs2.at[k], peer2(d)).start()
        between()
        whole = s2.at[k, pl.ds(0, 15)]
        done2 = rcopy(whole, whole, ss2.at[k], rs2.at[k], ring1((q1 + 1) % 4))
        done2.wait_recv()
        total = s2[k, 0]
        for j in range(1, 16):
            total = total + s2[k, j]
        done1.wait_send()
        done2.wait_send()
        return jnp.sum(total, axis=1, keepdims=True)

    def level_from(square):
        return jnp.sqrt(jnp.maximum(square, 0.0) / TOTAL + 1e-06)

    pl.semaphore_wait(barrier, 22)

    def begin():
        each(0, 4, y_send)
        s1_mask.start()
        each(0, TILES, lambda t: s1_obs(t).start())

    each(AHEAD, CHUNKS - 1, lambda i: ahead(i).start())
    sums = all_reduce(0, pack(square), begin)
    lev[...] = jnp.broadcast_to(level_from(sums[0:1]), (8, 128))

    def cloud_store(t):
        cols = pl.ds(pl.multiple_of(t * TILE, TILE), TILE)
        return pltpu.make_async_copy(lay.at[t], cloud_out.at[:, cols], out_sem.at[1 + t])

    def v_store(t):
        rows = pl.ds(pl.multiple_of(t * TILE, TILE), TILE)
        return pltpu.make_async_copy(vio.at[t], v_out.at[rows], out_sem.at[1 + TILES + t])

    def weigh(k, t):
        hw[k, t] = weight(mh.at[k], t).astype(bf16)

    def set_halo(k):
        uhs[k] = left(uh[k])

    def cut(value, level):
        return jnp.minimum(jnp.maximum(value, -level), level)

    mine, other = 4 * core, 4 * (1 - core)

    def y_more(low, high):
        each(jnp.minimum(low, CHUNKS), jnp.minimum(high, CHUNKS), y_send)

    def iteration(it, _):
        level = lev[0:1, 0:1]
        final = it == ITERS - 1
        y0 = 4 + CHUNKS * it

        @pl.when(final)
        def _():
            y_mask(iy).wait_recv()
            z_mask.start()

        each(Z_MARKS[0] * it, 2 + (Z_MARKS[1] - 2) * it, z_send)
        copies = []
        for part in range(2):

            def grow(t, acc):
                hi, low = split(cut(r[t], level))
                v_hi = vs[t, pl.ds(part * 128, 128)]
                v_low = vs[t, pl.ds(TILE + part * 128, 128)]
                both = mm_nt(hi, jnp.concatenate([v_hi, v_low], axis=0))
                return acc + both[:, :128] + both[:, 128:] + mm_nt(low, v_hi)

            gp[part] = lax.fori_loop(0, TILES, grow, jnp.zeros((TILE, 128), f32))
            copies.append(rcopy(gp.at[part], gr.at[part], gss.at[part], grs.at[part], col_pair))
            copies[-1].start()
        each(2 + (Z_MARKS[1] - 2) * it, 4 + (Z_MARKS[2] - 4) * it, z_send)
        for copy in copies:
            copy.wait()
        g = jnp.concatenate([gp[0] + gr[0], gp[1] + gr[1]], axis=1)
        gt[...] = g
        gs[...] = left(g)

        def curve(t, acc):
            c_t = w[t] * mm(gs[...], vs[t])
            c[t] = c_t
            return acc + fold(c_t * c_t)

        bottom = lax.fori_loop(0, TILES, curve, zero)

        @pl.when(it == 0)
        def _():
            ahead(CHUNKS - 1).start()

        def mask_out():
            @pl.when(it == 0)
            def _():
                y_mask(iz).start()

        sums = all_reduce(1 + 2 * it, pack(fold(g * g) * 0.5, bottom), mask_out)
        step = sums[0:1] / sums[1:2]
        set_u(u[...] + step * gt[...])
        uts[...] = left(jnp.transpose(u[...]))

        @pl.when(final)
        def _():
            y_pix(iz).start()
            s1_pix.start()

            def cross(i):
                ahead(i).wait_recv()
                across(i, iy).start()

            each(AHEAD, CHUNKS, cross)

        y_more(y0, y0 + 3)

        def pull(t):
            r_t, ac = r[t], step * c[t]
            r[t] = r_t - ac
            hp[t] = mm(uts[...], right(cut(r_t, level) - ac))

        def order(i):
            return jnp.where(i == 0, 2, jnp.where(i == 1, 1, jnp.where(i == 2, 3, 0)))

        def hand(k, slot):
            return rcopy(hp.at[other + k], hsib.at[slot], sibs.at[slot], sibr.at[slot], sibling)

        def reduce1(d):
            return rcopy(hp.at[mine + (q1 + d) % 4], n1.at[d - 1], r1s.at[d - 1], r1r.at[d - 1], ring1((q1 + d) % 4))

        def pull_step(i):
            @pl.when(i < 4)
            def _():
                d = order(i)
                pull(other + (q2 + d) % 4)
                hand((q2 + d) % 4, d).start()
                pull(mine + (q1 + d) % 4)

            @pl.when(i >= 1)
            def _():
                d = order(i - 1)
                hand(0, d).wait_recv()
                tile = mine + (q1 + d) % 4
                hp[tile] = hp[tile] + hsib[d]

                @pl.when(i < 4)
                def _():
                    reduce1(d).start()

        each(0, 5, pull_step)

        def base(k):
            set_halo(k)

            def step(t):
                low_rank[k, t] = mm(uhs[k], vs[t])

            each(0, TILES, step)

        @pl.when(it == 0)
        def _():
            s1_mask.wait_recv()
            each(0, TILES, lambda t: weigh(0, t))

        @pl.when(final)
        def _():
            s1_pix.wait_recv()
            base(0)

            def turn(t):
                vio[t] = jnp.transpose(vt[t])

            each(0, TILES, turn)

        for d in (1, 3, 2):
            reduce1(d).wait_recv()
        tile = mine + q1
        hp[tile] = hp[tile] + n1[0] + n1[1] + n1[2]

        j2 = q2 * 2 + h

        def sub(ref, j):
            return ref.at[tile, pl.ds(pl.multiple_of(32 * j, 32), 32)]

        def reduce2(e):
            j = (j2 + e) % 8
            return rcopy(sub(hp, j), n2.at[e - 1], r2s.at[e - 1], r2r.at[e - 1], ring2(j // 2, j % 2))

        for e in range(1, 8):
            reduce2(e).start()

        @pl.when(final)
        def _():
            y_pix(iy).wait_recv()
            z_pix.start()
            z_mask.wait_recv()
            s2_mask.start()
            base(iy)
            each(0, TILES, lambda t: weigh(2, t))
            each(0, TILES, lambda t: weigh(3, t))

        each(4, jnp.where(final, 4, Z_MARKS[0] - 1), z_send)
        for e in range(1, 8):
            reduce2(e).wait_recv()
        piece = sub(hp, j2)[...]
        for e in range(7):
            piece = piece + n2[e]
        sub(hf, j2)[...] = piece
        norm = fold(piece * piece)

        def gather2(e, j):
            to = (j2 + e) % 8
            return rcopy(sub(hf, j), sub(hf, j), a2s.at[e - 1], a2r.at[e - 1], ring2(to // 2, to % 2))

        def gather1(d, k):
            return rcopy(hf.at[mine + k], hf.at[mine + k], a1s.at[d - 1], a1r.at[d - 1], ring1((q1 + d) % 4))

        def onward(j):
            for d in (2, 1, 3):
                piece = sub(hf, j)
                rcopy(piece, piece, a1s.at[d - 1], a1r.at[d - 1], ring1((q1 + d) % 4)).start()

        for e in (2, 6, 4, 1, 7, 3, 5):
            gather2(e, j2).start()
        onward(j2)
        y_more(y0 + 3, y0 + 9)
        for e in (2, 6, 4, 1, 7, 3, 5):
            j = (j2 + 8 - e) % 8
            gather2(e, j).wait_recv()
            onward(j)

        def pass_on(k, i, half):
            return rcopy(hf.at[half + k], hf.at[half + k], fs.at[i], fr.at[i], sibling)

        pass_on(q1, 0, mine).start()

        @pl.when(final)
        def _():
            z_pix.wait_recv()
            s2_pix.start()
            base(iz)
            s2_pix.wait_recv()
            base(1)
            s2_mask.wait_recv()
            each(0, TILES, lambda t: weigh(1, t))

        def shift(t, accs):
            s_t = w[t] * mm(us[...], right(hf[t]))
            c[t] = s_t
            r_t = r[t]
            a0, a1, a2 = accs
            return a0 + fold(r_t * r_t), a1 + fold(r_t * s_t), a2 + fold(s_t * s_t)

        def arrival(i):
            return jnp.where(i == 2, 3, jnp.where(i == 3, 2, i))

        def shift_other(i, accs):
            k = (q2 + 4 - arrival(i)) % 4
            pass_on(k, i, other).wait_recv()
            return shift(other + k, accs)

        def shift_step(i, accs):
            d = arrival(i)
            k = (q1 + 4 - d) % 4
            gather1(d, k).wait_recv()
            pass_on(k, i, mine).start()
            return shift_other(i - 1, shift(mine + k, accs))

        accs = lax.fori_loop(1, 4, shift_step, shift(mine + q1, (zero, zero, zero)))
        accs = shift_other(3, accs)
        for d in (1, 2, 3):
            reduce1(d).wait_send()
            gather1(d, q1).wait_send()
        for e in range(1, 8):
            reduce2(e).wait_send()
            gather2(e, j2).wait_send()
        for i in range(4):
            hand(i, i).wait_send()
            pass_on(i, i, mine).wait_send()
        def meanwhile():
            y_more(y0 + 9, y0 + 12)

            @pl.when(final)
            def _():
                each(1, 4, halo_shift)

        def halo_shift(k):
            def step(t):
                low_shift[k, t] = mm(uhs[k], right(hf[t]))

            each(0, TILES, step)

        def turn_shift(t):
            lay[t] = jnp.transpose(hf[t])

        def early():
            @pl.when(final)
            def _():
                halo_shift(0)
                each(0, TILES, turn_shift)

        @pl.when(it == 0)
        def _():
            z_send(Z_MARKS[0] - 1)

        sums = all_reduce(2 + 2 * it, pack(norm, *accs), meanwhile, early)
        step = sums[0:1] / sums[3:4]
        square = sums[1:2] - 2.0 * step * sums[2:3] + step * step * sums[3:4]
        lev[...] = jnp.broadcast_to(level_from(square), (8, 128))

        @pl.when(final)
        def _():
            each(Z_MARKS[2], AHEAD, z_send)

        def update(t):
            v_t = vt[t] + step * hf[t]
            vt[t] = v_t
            vs[t] = right(v_t)
            r[t] = r[t] - step * c[t]

            @pl.when(final)
            def _():
                vio[t] = vio[t] + step * lay[t]
                v_store(t).start()

        each(0, TILES, update)
        lev2[...] = jnp.broadcast_to(step, (8, 128))
        return 0

    lax.fori_loop(0, ITERS, iteration, 0)
    stores = [pltpu.make_async_copy(u, u_out, out_sem.at[0])]
    stores[0].start()

    level = lev[0:1, 0:1]
    step_col = lev2[0:1, 0:1]
    inverse = 1.0 / level
    last = 63
    side = 1 - 2 * core

    def flag(offset):
        row = p + offset
        return ((row >= 0) & (row <= last)).astype(f32)

    has1, has2, has3 = flag(-side), flag(2 * side), flag(-2 * side)

    def soft(scaled):
        return scaled - jnp.minimum(jnp.maximum(scaled, -1.0), 1.0)

    def g(e):
        return e / (1.0 + e * e)

    def arrived(i):
        @pl.when(i < AHEAD)
        def _():
            z_obs(i).wait_recv()

        @pl.when(i >= AHEAD)
        def _():
            y_obs(i, iy).wait_recv()
            across(i, iz).wait_recv()

    def ready(t):
        each(2 * t, 2 * t + 2, arrived)
        s2_obs(t).start()

    STRIP = 32
    AT = 8

    def rim(ref):
        ref[AT - 1 : AT, :] = ref[AT : AT + 1, :]
        ref[AT + WIDTH : AT + WIDTH + 1, :] = ref[AT + WIDTH - 1 : AT + WIDTH, :]

    def along(src, dst):
        for at in range(AT, AT + WIDTH, STRIP):
            dst[pl.ds(at, STRIP), :] = g(src[pl.ds(at + 1, STRIP), :] - src[pl.ds(at, STRIP), :])

    def smooth_tile(t):
        @pl.when(t + 1 < TILES)
        def _():
            ready(t + 1)

        s1_obs(t).wait_recv()
        s2_obs(t).wait_recv()

        def halo(k, at):
            rows = pl.ds(at, STRIP)
            r_k = hx[k, t, rows, :] - low_rank[k, t, rows, :] - step_col * low_shift[k, t, rows, :]
            return hw[k, t, rows, :].astype(f32) * soft(r_k * inverse)

        for at in range(0, WIDTH, STRIP):
            rows = pl.ds(at + AT, STRIP)
            ya[2, rows, :] = soft(r[t, pl.ds(at, STRIP), :] * inverse)
            ya[0, rows, :] = halo(0, at)
            ya[1, rows, :] = halo(1, at)
        for row in range(3):
            rim(ya.at[row])
            along(ya.at[row], fb.at[row])

        def net(row, at):
            return fb[row, pl.ds(at + AT, STRIP), :] - fb[row, pl.ds(at + AT - 1, STRIP), :]

        for at in range(0, WIDTH, STRIP):
            rows = pl.ds(at + AT, STRIP)
            y0, y1, own = [ya[k, rows, :] for k in range(3)]
            to0 = g(y0 - own)
            to1 = g(has1 * (y1 - own))
            yb[2, rows, :] = own + diffusion * (to0 + to1 + net(2, at))
            yb[0, rows, :] = y0 + diffusion * (g(has2 * (halo(2, at) - y0)) - to0 + net(0, at))
            yb[1, rows, :] = y1 + diffusion * (g(has3 * (halo(3, at) - y1)) - to1 + net(1, at))
        rim(yb.at[2])
        along(yb.at[2], fb.at[2])
        for at in range(0, WIDTH, STRIP):
            rows = pl.ds(at + AT, STRIP)
            own = yb[2, rows, :]
            total = g(yb[0, rows, :] - own) + g(has1 * (yb[1, rows, :] - own)) + net(2, at)
            lay[t, pl.ds(at, STRIP), :] = level * (own + diffusion * total)
        cloud_store(t).start()

    for row in range(3):
        fb[row, :AT, :] = jnp.zeros((AT, TILE), f32)
    ready(0)
    each(0, TILES, smooth_tile)
    stores[0].wait()
    y_mask(iz).wait_send()
    y_pix(iz).wait_send()
    for copy in (z_mask, z_pix, s1_mask, s1_pix, s2_mask, s2_pix):
        copy.wait_send()

    def drain(i):
        y_obs(i, iz).wait_send()

        @pl.when(i < AHEAD)
        def _():
            z_obs(i).wait_send()

        @pl.when(i >= AHEAD)
        def _():
            ahead(i).wait_send()
            across(i, iy).wait_send()

    each(0, CHUNKS, drain)

    def close(t):
        s1_obs(t).wait_send()
        s2_obs(t).wait_send()
        cloud_store(t).wait()
        v_store(t).wait()

    each(0, TILES, close)


def hand_out(u_in, v_in, c_in, u_out, v_out, c_out, ub, vb, cb, load_sem, store_sem):
    moves = [(u_in, ub, u_out)]
    for i in range(4):
        rows = pl.ds(512 * i, 512)
        moves.append((v_in.at[rows], vb.at[rows], v_out.at[rows]))
        rows = pl.ds(64 * i, 64)
        moves.append((c_in.at[rows], cb.at[rows], c_out.at[rows]))
    loads = [pltpu.make_async_copy(a, b, load_sem.at[i]) for i, (a, b, _) in enumerate(moves)]
    stores = [pltpu.make_async_copy(b, c, store_sem.at[i]) for i, (_, b, c) in enumerate(moves)]
    for load in loads:
        load.start()
    for load, store in zip(loads, stores):
        load.wait()
        store.start()
    for store in stores:
        store.wait()


def per_device(observed, valid_mask, pix_factor, col_factor):
    any_space = pl.BlockSpec(memory_space=pl.ANY)
    full = pltpu.VMEM((TILES, TILE, TILE), f32)
    square = pltpu.VMEM((TILE, TILE), f32)
    pair = pltpu.VMEM((TILE, 3 * TILE), bf16)
    dma = pltpu.SemaphoreType.DMA
    shapes = (
        jax.ShapeDtypeStruct((256, 256), f32),
        jax.ShapeDtypeStruct((2048, 256), f32),
        jax.ShapeDtypeStruct((256, 2048), f32),
    )
    results = pl.pallas_call(
        kernel,
        out_shape=shapes,
        in_specs=[any_space] * 4,
        out_specs=[any_space] * 3,
        scratch_shapes=[
            full, full, full, full,
            pltpu.VMEM((TILES, 3 * TILE, TILE), bf16),
            full,
            pltpu.VMEM((4, TILE, TILE), f32),
            full, full, full,
            pltpu.VMEM((256, 256), jnp.int32),
            pltpu.VMEM((4, 128, TILE), bf16),
            square, pair, pair,
            pltpu.VMEM((2, TILE, 128), f32), pltpu.VMEM((2, TILE, 128), f32),
            square, pair,
            pltpu.VMEM((3, TILE, TILE), f32),
            pltpu.VMEM((7, 32, TILE), f32),
            pltpu.VMEM((5, 8, 4, 128), f32),
            pltpu.VMEM((5, 16, 4, 128), f32),
            pltpu.VMEM((8, 128), f32),
            pltpu.VMEM((4, TILES, TILE, TILE), f32),
            pltpu.VMEM((4, 256, 256), jnp.int32),
            pltpu.VMEM((4, TILE, TILE), f32),
            pltpu.VMEM((4, TILE, 3 * TILE), bf16),
            pltpu.VMEM((4, TILES, TILE, TILE), f32),
            pltpu.VMEM((4, TILES, TILE, TILE), f32),
            pltpu.VMEM((8, 128), f32),
            pltpu.VMEM((4, TILES, TILE, TILE), bf16),
            pltpu.VMEM((CHUNKS - AHEAD, 128, TILE), f32),
            pltpu.VMEM((3, TILE + 16, TILE), f32),
            pltpu.VMEM((3, TILE + 16, TILE), f32),
            pltpu.VMEM((3, TILE + 16, TILE), f32),
            dma((2 * TILES + 2,)), dma((2 * TILES + 1,)),
            dma((5,)), dma((5,)), dma((5,)), dma((5,)),
            dma((2,)), dma((2,)), dma((4,)), dma((4,)),
            dma((3,)), dma((3,)), dma((7,)), dma((7,)),
            dma((7,)), dma((7,)), dma((3,)), dma((3,)), dma((4,)), dma((4,)),
            dma((3,)), dma((3,)), dma((3,)), dma((3,)),
            dma((CHUNKS + 2,)), dma((CHUNKS + 2,)), dma((CHUNKS + 2,)), dma((CHUNKS + 2,)),
            dma((TILES + 2,)), dma((TILES + 2,)), dma((TILES + 2,)), dma((TILES + 2,)),
        ],
        compiler_params=pltpu.CompilerParams(
            collective_id=0, has_side_effects=True, vmem_limit_bytes=60 * 1024 * 1024
        ),
        name="separate",
    )(observed, valid_mask, pix_factor, col_factor)
    return pl.pallas_call(
        hand_out,
        out_shape=shapes,
        in_specs=[any_space] * 3,
        out_specs=[any_space] * 3,
        scratch_shapes=[
            square,
            pltpu.VMEM((2048, 256), f32),
            pltpu.VMEM((256, 2048), f32),
            dma((9,)), dma((9,)),
        ],
        compiler_params=pltpu.CompilerParams(vmem_limit_bytes=60 * 1024 * 1024),
        name="hand_out",
    )(*results)


def solution(mesh):
    in_specs = (P("pix", "col"), P("pix", "col"), P("pix", None), P("col", None))
    out_specs = (P("pix", None), P("col", None), P("pix", "col"))
    return jax.shard_map(
        per_device, mesh=mesh, in_specs=in_specs, out_specs=out_specs, check_vma=False
    )
```

time: 197 us -> 179 us (0.909)
  Pallas kernels: 190 us -> 179 us
  local copies, waits for them, and re-layouts: 6.19 us -> 0 us
    pallas_call x1 -> x2, Pallas kernels: 190 us -> 179 us  [the longest x1 175 us: per_device(): pl.pallas_call(kernel, out_shape=shapes, in_specs=[any_space] * 4, out_sp...]
    unnamed x5 -> x0, local copies, waits for them, and re-layouts: 6.19 us -> none
where the time goes in v3:
time: 179 us
  Pallas kernels  179 us (100%)
    pallas_call x1, Pallas kernels, per_device(): pl.pallas_call(kernel, out_shape=shapes, in_specs=[any_space] * 4, out_sp...  175 us
    pallas_call x1, Pallas kernels, per_device(): pl.pallas_call(hand_out, out_shape=shapes, in_specs=[any_space] * 3, out_...  4.01 us

profile of v3, /device:TPU:1, one launch (start us, length us, event | category | flops | bytes accessed | tf_op | source)
XLA Modules:
  0.0 179.3 jit_solution(8985741553877167320)
XLA Ops:
  0.6 174.7 %separate.1 = (f32[256,256]{1,0:T(8,128)}, f32[2048,256]{1,0:T(8,128)}, f32[256,2048]{1,0:T(8,128)}) custom-call(f32[256,2048]{1,0:T(8,128)} %obs_in.1, s32[256,256]{1,0:T(8,128)} %mask_in.1, f32[256,256]{1,0:T(8,128)} %u_in.1, f32[2048,256]{1,0:T(8,128)} %v_in.1), custom_call_target="tpu_custom_call" | custom-call | tf_op jit(solution)/shard_map/separate/pallas_call | solution.py:708
  175.3 4.0 %hand_out.1 = (f32[256,256]{1,0:T(8,128)}, f32[2048,256]{1,0:T(8,128)}, f32[256,2048]{1,0:T(8,128)}) custom-call(f32[256,256]{1,0:T(8,128)} %get-tuple-element.6.u_in, f32[2048,256]{1,0:T(8,128)} %get-tuple-element.7.v_in, f32[256,2048]{1,0:T(8,128)} %get-tuple-element.8.c_in), custom_call_target="tpu_custom_call" | custom-call | tf_op jit(solution)/shard_map/hand_out/pallas_call | solution.py:755

commit v4 on v3

--- a/solution.py
+++ b/solution.py
@@ -11,8 +11,8 @@
 TILE = 256
 TILES = 8
 CHUNKS = 16
-Z_MARKS = (6, 7, 10)
-AHEAD = 13
+Z_MARKS = (5, 6, 9)
+AHEAD = 11
 
 TOTAL = 67108864.0
 diffusion = 0.2
@@ -58,11 +58,11 @@
 
 def kernel(
     obs_in, mask_in, u_in, v_in,
-    u_out, v_out, cloud_out,
-    r, w, c, vt, vs, hp, hsib, hf, vio, lay, mask, spread,
+    u_out, vio, lay,
+    r, w, c, vt, vs, hp, hsib, hf, mask, spread,
     u, us, uts, gp, gr, gt, gs, n1, n2, s1, s2, lev,
-    hx, mh, uh, uhs, low_rank, low_shift, lev2, hw, way, ya, yb, fb,
-    in_sem, out_sem, ss1, rs1, ss2, rs2, gss, grs, sibs, sibr,
+    hx, mh, uh, uhs, low_rank, low_shift, lev2, hw, way, ya, yb, yc, y_sib, p_sib, p_far, fb,
+    in_sem, ss1, rs1, ss2, rs2, gss, grs, sibs, sibr,
     r1s, r1r, r2s, r2r, a2s, a2r, a1s, a1r, fs, fr,
     was, war, wbs, wbr, hys, hyr, hzs, hzr, h1s, h1r, h2s, h2r,
 ):
@@ -90,8 +90,8 @@
     z_next = peer2(17 - 2 * h)
     q1 = x + core * (z - x)
     q2 = z + core * (x - z)
-    iy = 2 + (h + core) % 2
-    iz = 5 - iy
+    iy = 1 + (h + core) % 2
+    iz = 3 - iy
 
     def ring1(q):
         return dev(q + core * (x - q), z + core * (q - z), h, core, lo)
@@ -170,18 +170,20 @@
 
     z_mask = rcopy(mh.at[iy], mh.at[iz], hzs.at[MASK], hzr.at[MASK], z_next)
     z_pix = rcopy(uh.at[iy], uh.at[iz], hzs.at[PIX], hzr.at[PIX], z_next)
-    s1_mask = rcopy(mask_in, mh.at[0], h1s.at[TILES], h1r.at[TILES], sibling)
-    s1_pix = rcopy(u, uh.at[0], h1s.at[TILES + 1], h1r.at[TILES + 1], sibling)
-
-    def s1_obs(t):
-        cols = pl.ds(pl.multiple_of(t * TILE, TILE), TILE)
-        return rcopy(obs_in.at[:, cols], hx.at[0, t], h1s.at[t], h1r.at[t], sibling)
+    AT = 8
+    inner = pl.ds(AT, WIDTH)
+
+    def s1_layer(t):
+        return rcopy(ya.at[t, inner], y_sib.at[t], h1s.at[t], h1r.at[t], sibling)
+
+    def s1_pass(t):
+        return rcopy(yb.at[t, inner], p_sib.at[t], h1s.at[TILES + t], h1r.at[TILES + t], sibling)
 
     def s2_obs(t):
-        return rcopy(hx.at[2, t], hx.at[1, t], h2s.at[t], h2r.at[t], sibling)
-
-    s2_mask = rcopy(mh.at[2], mh.at[1], h2s.at[TILES], h2r.at[TILES], sibling)
-    s2_pix = rcopy(uh.at[2], uh.at[1], h2s.at[TILES + 1], h2r.at[TILES + 1], sibling)
+        return rcopy(hx.at[1, t], hx.at[0, t], h2s.at[t], h2r.at[t], sibling)
+
+    s2_mask = rcopy(mh.at[1], mh.at[0], h2s.at[TILES], h2r.at[TILES], sibling)
+    s2_pix = rcopy(uh.at[1], uh.at[0], h2s.at[TILES + 1], h2r.at[TILES + 1], sibling)
 
     for load in loads[: TILES]:
         load.wait()
@@ -214,6 +216,23 @@
 
     zero = jnp.zeros((8, 128), f32)
     square = lax.fori_loop(0, TILES, first, zero)
+
+    def arrived(i):
+        @pl.when(i < AHEAD)
+        def _():
+            z_obs(i).wait_recv()
+
+        @pl.when(i >= AHEAD)
+        def _():
+            y_obs(i, iy).wait_recv()
+            across(i, iz).wait_recv()
+
+    def ready(t):
+        each(2 * t, 2 * t + 2, arrived)
+        s2_obs(t).start()
+
+    def turn_of(i):
+        return (i + 6) % TILES
 
     def all_reduce(k, message, between, early=lambda: None):
         s1[k, i1] = message
@@ -246,27 +265,20 @@
     pl.semaphore_wait(barrier, 22)
 
     def begin():
-        each(0, 4, y_send)
-        s1_mask.start()
-        each(0, TILES, lambda t: s1_obs(t).start())
-
-    each(AHEAD, CHUNKS - 1, lambda i: ahead(i).start())
+        each(0, 3, y_send)
+
+    each(AHEAD, CHUNKS - 2, lambda i: ahead(i).start())
     sums = all_reduce(0, pack(square), begin)
     lev[...] = jnp.broadcast_to(level_from(sums[0:1]), (8, 128))
 
-    def cloud_store(t):
-        cols = pl.ds(pl.multiple_of(t * TILE, TILE), TILE)
-        return pltpu.make_async_copy(lay.at[t], cloud_out.at[:, cols], out_sem.at[1 + t])
-
-    def v_store(t):
-        rows = pl.ds(pl.multiple_of(t * TILE, TILE), TILE)
-        return pltpu.make_async_copy(vio.at[t], v_out.at[rows], out_sem.at[1 + TILES + t])
+    def soft(scaled):
+        return scaled - jnp.minimum(jnp.maximum(scaled, -1.0), 1.0)
 
     def weigh(k, t):
-        hw[k, t] = weight(mh.at[k], t).astype(bf16)
+        hw[k // 2, t] = weight(mh.at[k], t).astype(bf16)
 
     def set_halo(k):
-        uhs[k] = left(uh[k])
+        uhs[k // 2] = left(uh[k])
 
     def cut(value, level):
         return jnp.minimum(jnp.maximum(value, -level), level)
@@ -279,12 +291,16 @@
     def iteration(it, _):
         level = lev[0:1, 0:1]
         final = it == ITERS - 1
-        y0 = 4 + CHUNKS * it
+        y0 = 3 + CHUNKS * it
 
         @pl.when(final)
         def _():
             y_mask(iy).wait_recv()
             z_mask.start()
+
+        @pl.when(it == 0)
+        def _():
+            ahead(CHUNKS - 2).start()
 
         each(Z_MARKS[0] * it, 2 + (Z_MARKS[1] - 2) * it, z_send)
         copies = []
@@ -300,7 +316,7 @@
             gp[part] = lax.fori_loop(0, TILES, grow, jnp.zeros((TILE, 128), f32))
             copies.append(rcopy(gp.at[part], gr.at[part], gss.at[part], grs.at[part], col_pair))
             copies[-1].start()
-        each(2 + (Z_MARKS[1] - 2) * it, 4 + (Z_MARKS[2] - 4) * it, z_send)
+        each(2 + (Z_MARKS[1] - 2) * it, 3 + (Z_MARKS[2] - 3) * it, z_send)
         for copy in copies:
             copy.wait()
         g = jnp.concatenate([gp[0] + gr[0], gp[1] + gr[1]], axis=1)
@@ -318,10 +334,18 @@
         def _():
             ahead(CHUNKS - 1).start()
 
+        def cross(i):
+            ahead(i).wait_recv()
+            across(i, iy).start()
+
         def mask_out():
             @pl.when(it == 0)
             def _():
                 y_mask(iz).start()
+
+            @pl.when(final)
+            def _():
+                each(AHEAD, AHEAD + 2, cross)
 
         sums = all_reduce(1 + 2 * it, pack(fold(g * g) * 0.5, bottom), mask_out)
         step = sums[0:1] / sums[1:2]
@@ -331,15 +355,8 @@
         @pl.when(final)
         def _():
             y_pix(iz).start()
-            s1_pix.start()
-
-            def cross(i):
-                ahead(i).wait_recv()
-                across(i, iy).start()
-
-            each(AHEAD, CHUNKS, cross)
-
-        y_more(y0, y0 + 3)
+
+        y_more(y0, y0 + 4)
 
         def pull(t):
             r_t, ac = r[t], step * c[t]
@@ -380,20 +397,12 @@
             set_halo(k)
 
             def step(t):
-                low_rank[k, t] = mm(uhs[k], vs[t])
+                low_rank[k // 2, t] = mm(uhs[k // 2], vs[t])
 
             each(0, TILES, step)
 
-        @pl.when(it == 0)
-        def _():
-            s1_mask.wait_recv()
-            each(0, TILES, lambda t: weigh(0, t))
-
         @pl.when(final)
         def _():
-            s1_pix.wait_recv()
-            base(0)
-
             def turn(t):
                 vio[t] = jnp.transpose(vt[t])
 
@@ -422,11 +431,20 @@
             z_pix.start()
             z_mask.wait_recv()
             s2_mask.start()
-            base(iy)
             each(0, TILES, lambda t: weigh(2, t))
-            each(0, TILES, lambda t: weigh(3, t))
-
-        each(4, jnp.where(final, 4, Z_MARKS[0] - 1), z_send)
+
+            @pl.when(iy == 1)
+            def _():
+                s2_pix.start()
+
+            @pl.when(iy == 2)
+            def _():
+                base(2)
+
+            s2_mask.wait_recv()
+            each(0, TILES, lambda t: weigh(0, t))
+
+        each(3, jnp.where(final, 3, Z_MARKS[0] - 1), z_send)
         for e in range(1, 8):
             reduce2(e).wait_recv()
         piece = sub(hp, j2)[...]
@@ -450,7 +468,12 @@
         for e in (2, 6, 4, 1, 7, 3, 5):
             gather2(e, j2).start()
         onward(j2)
-        y_more(y0 + 3, y0 + 9)
+        y_more(y0 + 4, y0 + 10)
+
+        @pl.when(final)
+        def _():
+            each(AHEAD + 2, CHUNKS, cross)
+
         for e in (2, 6, 4, 1, 7, 3, 5):
             j = (j2 + 8 - e) % 8
             gather2(e, j).wait_recv()
@@ -464,12 +487,17 @@
         @pl.when(final)
         def _():
             z_pix.wait_recv()
-            s2_pix.start()
-            base(iz)
+
+            @pl.when(iy == 2)
+            def _():
+                s2_pix.start()
+
+            @pl.when(iy == 1)
+            def _():
+                base(2)
+
             s2_pix.wait_recv()
-            base(1)
-            s2_mask.wait_recv()
-            each(0, TILES, lambda t: weigh(1, t))
+            base(0)
 
         def shift(t, accs):
             s_t = w[t] * mm(us[...], right(hf[t]))
@@ -505,11 +533,13 @@
             hand(i, i).wait_send()
             pass_on(i, i, mine).wait_send()
         def meanwhile():
-            y_more(y0 + 9, y0 + 12)
+            y_more(y0 + 10, y0 + 13)
 
             @pl.when(final)
             def _():
-                each(1, 4, halo_shift)
+                each(0, 2, halo_shift)
+                ready(turn_of(0))
+                ready(turn_of(1))
 
         def halo_shift(k):
             def step(t):
@@ -523,7 +553,6 @@
         def early():
             @pl.when(final)
             def _():
-                halo_shift(0)
                 each(0, TILES, turn_shift)
 
         @pl.when(it == 0)
@@ -539,24 +568,27 @@
         def _():
             each(Z_MARKS[2], AHEAD, z_send)
 
+        inverse = 1.0 / level_from(square)
+
         def update(t):
             v_t = vt[t] + step * hf[t]
             vt[t] = v_t
             vs[t] = right(v_t)
-            r[t] = r[t] - step * c[t]
+            r_t = r[t] - step * c[t]
+            r[t] = r_t
 
             @pl.when(final)
             def _():
+                ya[t, inner, :] = soft(r_t * inverse)
+                s1_layer(t).start()
                 vio[t] = vio[t] + step * lay[t]
-                v_store(t).start()
 
         each(0, TILES, update)
         lev2[...] = jnp.broadcast_to(step, (8, 128))
         return 0
 
     lax.fori_loop(0, ITERS, iteration, 0)
-    stores = [pltpu.make_async_copy(u, u_out, out_sem.at[0])]
-    stores[0].start()
+    u_out[...] = u[...]
 
     level = lev[0:1, 0:1]
     step_col = lev2[0:1, 0:1]
@@ -568,89 +600,75 @@
         row = p + offset
         return ((row >= 0) & (row <= last)).astype(f32)
 
-    has1, has2, has3 = flag(-side), flag(2 * side), flag(-2 * side)
-
-    def soft(scaled):
-        return scaled - jnp.minimum(jnp.maximum(scaled, -1.0), 1.0)
+    has1, has2 = flag(-side), flag(-2 * side)
 
     def g(e):
         return e / (1.0 + e * e)
 
-    def arrived(i):
-        @pl.when(i < AHEAD)
-        def _():
-            z_obs(i).wait_recv()
-
-        @pl.when(i >= AHEAD)
-        def _():
-            y_obs(i, iy).wait_recv()
-            across(i, iz).wait_recv()
-
-    def ready(t):
-        each(2 * t, 2 * t + 2, arrived)
-        s2_obs(t).start()
-
     STRIP = 32
-    AT = 8
+    strips = range(0, WIDTH, STRIP)
 
     def rim(ref):
         ref[AT - 1 : AT, :] = ref[AT : AT + 1, :]
         ref[AT + WIDTH : AT + WIDTH + 1, :] = ref[AT + WIDTH - 1 : AT + WIDTH, :]
 
     def along(src, dst):
+        rim(src)
         for at in range(AT, AT + WIDTH, STRIP):
             dst[pl.ds(at, STRIP), :] = g(src[pl.ds(at + 1, STRIP), :] - src[pl.ds(at, STRIP), :])
 
-    def smooth_tile(t):
-        @pl.when(t + 1 < TILES)
-        def _():
-            ready(t + 1)
-
-        s1_obs(t).wait_recv()
+    def net(row, at):
+        return fb[row, pl.ds(at + AT, STRIP), :] - fb[row, pl.ds(at + AT - 1, STRIP), :]
+
+    def pass1(t):
         s2_obs(t).wait_recv()
 
         def halo(k, at):
             rows = pl.ds(at, STRIP)
-            r_k = hx[k, t, rows, :] - low_rank[k, t, rows, :] - step_col * low_shift[k, t, rows, :]
+            r_k = hx[2 * k, t, rows, :] - low_rank[k, t, rows, :] - step_col * low_shift[k, t, rows, :]
             return hw[k, t, rows, :].astype(f32) * soft(r_k * inverse)
 
-        for at in range(0, WIDTH, STRIP):
+        for at in strips:
+            yc[pl.ds(at + AT, STRIP), :] = halo(0, at)
+        along(ya.at[t], fb.at[0])
+        along(yc, fb.at[1])
+        s1_layer(t).wait_recv()
+        for at in strips:
             rows = pl.ds(at + AT, STRIP)
-            ya[2, rows, :] = soft(r[t, pl.ds(at, STRIP), :] * inverse)
-            ya[0, rows, :] = halo(0, at)
-            ya[1, rows, :] = halo(1, at)
-        for row in range(3):
-            rim(ya.at[row])
-            along(ya.at[row], fb.at[row])
-
-        def net(row, at):
-            return fb[row, pl.ds(at + AT, STRIP), :] - fb[row, pl.ds(at + AT - 1, STRIP), :]
-
-        for at in range(0, WIDTH, STRIP):
-            rows = pl.ds(at + AT, STRIP)
-            y0, y1, own = [ya[k, rows, :] for k in range(3)]
-            to0 = g(y0 - own)
+            own, y1 = ya[t, rows, :], yc[rows, :]
             to1 = g(has1 * (y1 - own))
-            yb[2, rows, :] = own + diffusion * (to0 + to1 + net(2, at))
-            yb[0, rows, :] = y0 + diffusion * (g(has2 * (halo(2, at) - y0)) - to0 + net(0, at))
-            yb[1, rows, :] = y1 + diffusion * (g(has3 * (halo(3, at) - y1)) - to1 + net(1, at))
-        rim(yb.at[2])
-        along(yb.at[2], fb.at[2])
-        for at in range(0, WIDTH, STRIP):
-            rows = pl.ds(at + AT, STRIP)
-            own = yb[2, rows, :]
-            total = g(yb[0, rows, :] - own) + g(has1 * (yb[1, rows, :] - own)) + net(2, at)
-            lay[t, pl.ds(at, STRIP), :] = level * (own + diffusion * total)
-        cloud_store(t).start()
+            yb[t, rows, :] = own + diffusion * (g(y_sib[t, pl.ds(at, STRIP), :] - own) + to1 + net(0, at))
+            p_far[t, pl.ds(at, STRIP), :] = y1 + diffusion * (g(has2 * (halo(1, at) - y1)) - to1 + net(1, at))
+        s1_pass(t).start()
+
+    def pass2(t):
+        along(yb.at[t], fb.at[2])
+        s1_pass(t).wait_recv()
+        for at in strips:
+            rows = pl.ds(at, STRIP)
+            own = yb[t, pl.ds(at + AT, STRIP), :]
+            total = g(p_sib[t, rows, :] - own) + g(has1 * (p_far[t, rows, :] - own)) + net(2, at)
+            lay[t, rows, :] = level * (own + diffusion * total)
+
+    def smooth_tile(i):
+        @pl.when(i < TILES)
+        def _():
+            @pl.when(i + 2 < TILES)
+            def _():
+                ready(turn_of(i + 2))
+
+            pass1(turn_of(i))
+
+        @pl.when(i > 1)
+        def _():
+            pass2(turn_of(i - 2))
 
     for row in range(3):
         fb[row, :AT, :] = jnp.zeros((AT, TILE), f32)
-    ready(0)
-    each(0, TILES, smooth_tile)
-    stores[0].wait()
+    each(0, TILES + 2, smooth_tile)
     y_mask(iz).wait_send()
     y_pix(iz).wait_send()
-    for copy in (z_mask, z_pix, s1_mask, s1_pix, s2_mask, s2_pix):
+    for copy in (z_mask, z_pix, s2_mask, s2_pix):
         copy.wait_send()
 
     def drain(i):
@@ -668,27 +686,20 @@
     each(0, CHUNKS, drain)
 
     def close(t):
-        s1_obs(t).wait_send()
+        s1_layer(t).wait_send()
+        s1_pass(t).wait_send()
         s2_obs(t).wait_send()
-        cloud_store(t).wait()
-        v_store(t).wait()
 
     each(0, TILES, close)
 
 
-def hand_out(u_in, v_in, c_in, u_out, v_out, c_out, ub, vb, cb, load_sem, store_sem):
-    moves = [(u_in, ub, u_out)]
-    for i in range(4):
-        rows = pl.ds(512 * i, 512)
-        moves.append((v_in.at[rows], vb.at[rows], v_out.at[rows]))
-        rows = pl.ds(64 * i, 64)
-        moves.append((c_in.at[rows], cb.at[rows], c_out.at[rows]))
-    loads = [pltpu.make_async_copy(a, b, load_sem.at[i]) for i, (a, b, _) in enumerate(moves)]
-    stores = [pltpu.make_async_copy(b, c, store_sem.at[i]) for i, (_, b, c) in enumerate(moves)]
-    for load in loads:
-        load.start()
-    for load, store in zip(loads, stores):
-        load.wait()
+def hand_out(u_in, v_in, c_in, u_out, v_out, c_out, sem):
+    moves = [(u_in, u_out)]
+    for t in range(TILES):
+        span = pl.ds(t * TILE, TILE)
+        moves += [(v_in.at[t], v_out.at[span]), (c_in.at[t], c_out.at[:, span])]
+    stores = [pltpu.make_async_copy(a, b, sem.at[i]) for i, (a, b) in enumerate(moves)]
+    for store in stores:
         store.start()
     for store in stores:
         store.wait()
@@ -707,15 +718,19 @@
     )
     results = pl.pallas_call(
         kernel,
-        out_shape=shapes,
+        out_shape=(
+            pltpu.VMEM((TILE, TILE), f32),
+            pltpu.VMEM((TILES, TILE, TILE), f32),
+            pltpu.VMEM((TILES, TILE, TILE), f32),
+        ),
         in_specs=[any_space] * 4,
-        out_specs=[any_space] * 3,
+        out_specs=[pl.BlockSpec(memory_space=pltpu.VMEM)] * 3,
         scratch_shapes=[
             full, full, full, full,
             pltpu.VMEM((TILES, 3 * TILE, TILE), bf16),
             full,
             pltpu.VMEM((4, TILE, TILE), f32),
-            full, full, full,
+            full,
             pltpu.VMEM((256, 256), jnp.int32),
             pltpu.VMEM((4, 128, TILE), bf16),
             square, pair, pair,
@@ -726,44 +741,42 @@
             pltpu.VMEM((5, 8, 4, 128), f32),
             pltpu.VMEM((5, 16, 4, 128), f32),
             pltpu.VMEM((8, 128), f32),
-            pltpu.VMEM((4, TILES, TILE, TILE), f32),
-            pltpu.VMEM((4, 256, 256), jnp.int32),
-            pltpu.VMEM((4, TILE, TILE), f32),
-            pltpu.VMEM((4, TILE, 3 * TILE), bf16),
-            pltpu.VMEM((4, TILES, TILE, TILE), f32),
-            pltpu.VMEM((4, TILES, TILE, TILE), f32),
+            pltpu.VMEM((3, TILES, TILE, TILE), f32),
+            pltpu.VMEM((3, 256, 256), jnp.int32),
+            pltpu.VMEM((3, TILE, TILE), f32),
+            pltpu.VMEM((2, TILE, 3 * TILE), bf16),
+            pltpu.VMEM((2, TILES, TILE, TILE), f32),
+            pltpu.VMEM((2, TILES, TILE, TILE), f32),
             pltpu.VMEM((8, 128), f32),
-            pltpu.VMEM((4, TILES, TILE, TILE), bf16),
+            pltpu.VMEM((2, TILES, TILE, TILE), bf16),
             pltpu.VMEM((CHUNKS - AHEAD, 128, TILE), f32),
+            pltpu.VMEM((TILES, TILE + 16, TILE), f32),
+            pltpu.VMEM((TILES, TILE + 16, TILE), f32),
+            pltpu.VMEM((TILE + 16, TILE), f32),
+            full, full,
+            full,
             pltpu.VMEM((3, TILE + 16, TILE), f32),
-            pltpu.VMEM((3, TILE + 16, TILE), f32),
-            pltpu.VMEM((3, TILE + 16, TILE), f32),
-            dma((2 * TILES + 2,)), dma((2 * TILES + 1,)),
+            dma((2 * TILES + 2,)),
             dma((5,)), dma((5,)), dma((5,)), dma((5,)),
             dma((2,)), dma((2,)), dma((4,)), dma((4,)),
             dma((3,)), dma((3,)), dma((7,)), dma((7,)),
             dma((7,)), dma((7,)), dma((3,)), dma((3,)), dma((4,)), dma((4,)),
-            dma((3,)), dma((3,)), dma((3,)), dma((3,)),
+            dma((5,)), dma((5,)), dma((5,)), dma((5,)),
             dma((CHUNKS + 2,)), dma((CHUNKS + 2,)), dma((CHUNKS + 2,)), dma((CHUNKS + 2,)),
-            dma((TILES + 2,)), dma((TILES + 2,)), dma((TILES + 2,)), dma((TILES + 2,)),
+            dma((2 * TILES,)), dma((2 * TILES,)), dma((TILES + 2,)), dma((TILES + 2,)),
         ],
         compiler_params=pltpu.CompilerParams(
-            collective_id=0, has_side_effects=True, vmem_limit_bytes=60 * 1024 * 1024
+            collective_id=0, has_side_effects=True, vmem_limit_bytes=57 * 1024 * 1024
         ),
         name="separate",
     )(observed, valid_mask, pix_factor, col_factor)
     return pl.pallas_call(
         hand_out,
         out_shape=shapes,
-        in_specs=[any_space] * 3,
+        in_specs=[pl.BlockSpec(memory_space=pltpu.VMEM)] * 3,
         out_specs=[any_space] * 3,
-        scratch_shapes=[
-            square,
-            pltpu.VMEM((2048, 256), f32),
-            pltpu.VMEM((256, 2048), f32),
-            dma((9,)), dma((9,)),
-        ],
-        compiler_params=pltpu.CompilerParams(vmem_limit_bytes=60 * 1024 * 1024),
+        scratch_shapes=[dma((2 * TILES + 1,))],
+        compiler_params=pltpu.CompilerParams(vmem_limit_bytes=16 * 1024 * 1024),
         name="hand_out",
     )(*results)
 

time: 179 us -> 172 us (0.961)
  Pallas kernels: 179 us -> 172 us
    pallas_call x2, Pallas kernels: 179 us -> 172 us  [the longest x1 169 us: per_device(): pl.pallas_call(kernel, out_shape=(pltpu.VMEM((TILE, TILE), f32), pltpu.VM...]
where the time goes in v4:
time: 172 us
  Pallas kernels  172 us (100%)
    pallas_call x1, Pallas kernels, per_device(): pl.pallas_call(kernel, out_shape=(pltpu.VMEM((TILE, TILE), f32), pltpu.VM...  169 us

profile of v4, /device:TPU:1, one launch (start us, length us, event | category | flops | bytes accessed | tf_op | source)
XLA Modules:
  0.0 172.3 jit_solution(7211321453622924044)
XLA Ops:
  0.6 169.5 %separate.1 = (f32[256,256]{1,0:T(8,128)S(1)}, f32[8,256,256]{2,1,0:T(8,128)S(1)}, f32[8,256,256]{2,1,0:T(8,128)S(1)}) custom-call(f32[256,2048]{1,0:T(8,128)} %obs_in.1, s32[256,256]{1,0:T(8,128)} %mask_in.1, f32[256,256]{1,0:T(8,128)} %u_in.1, f32[2048,256]{1,0:T(8,128)} %v_in.1), custom_call_target="tpu_custom_call" | custom-call | tf_op jit(solution)/shard_map/separate/pallas_call | solution.py:719
  170.1 2.2 %hand_out.1 = (f32[256,256]{1,0:T(8,128)}, f32[2048,256]{1,0:T(8,128)}, f32[256,2048]{1,0:T(8,128)}) custom-call(f32[256,256]{1,0:T(8,128)S(1)} %get-tuple-element.6.u_in, f32[8,256,256]{2,1,0:T(8,128)S(1)} %get-tuple-element.7.v_in, f32[8,256,256]{2,1,0:T(8,128)S(1)} %get-tuple-element.8.c_in), custom_call_target="tpu_custom_call" | custom-call | tf_op jit(solution)/shard_map/hand_out/pallas_call | solution.py:773

commit v5 on v4

--- a/solution.py
+++ b/solution.py
@@ -11,7 +11,7 @@
 TILE = 256
 TILES = 8
 CHUNKS = 16
-Z_MARKS = (5, 6, 9)
+Z_MARKS = (4, 5, 8)
 AHEAD = 11
 
 TOTAL = 67108864.0
@@ -155,7 +155,8 @@
         t, rows = chunk(i)
         return rcopy(way.at[i - AHEAD], hx.at[slot, t, rows], wbs.at[i - AHEAD], wbr.at[i - AHEAD], y_pair)
 
-    def y_send(i):
+    def y_send(j):
+        i = jnp.where(j < 9, j, jnp.where(j < 13, j + 3, j - 4))
         y_obs(i, iz).start()
 
     def z_send(i):
@@ -345,7 +346,8 @@
 
             @pl.when(final)
             def _():
-                each(AHEAD, AHEAD + 2, cross)
+                each(AHEAD + 4, CHUNKS, cross)
+                y_send(12)
 
         sums = all_reduce(1 + 2 * it, pack(fold(g * g) * 0.5, bottom), mask_out)
         step = sums[0:1] / sums[1:2]
@@ -355,8 +357,9 @@
         @pl.when(final)
         def _():
             y_pix(iz).start()
-
-        y_more(y0, y0 + 4)
+            cross(AHEAD + 3)
+
+        y_more(y0, y0 + 3)
 
         def pull(t):
             r_t, ac = r[t], step * c[t]
@@ -396,17 +399,18 @@
         def base(k):
             set_halo(k)
 
-            def step(t):
-                low_rank[k // 2, t] = mm(uhs[k // 2], vs[t])
-
-            each(0, TILES, step)
+            each(0, TILES, lambda t: base_tile(k, t))
+
+        def base_tile(k, t):
+            low_rank[k // 2, t] = mm(uhs[k // 2], vs[t])
 
         @pl.when(final)
         def _():
-            def turn(t):
-                vio[t] = jnp.transpose(vt[t])
-
-            each(0, TILES, turn)
+            z_mask.wait_recv()
+            s2_mask.start()
+            each(0, TILES, lambda t: weigh(2, t))
+            s2_mask.wait_recv()
+            each(0, TILES, lambda t: weigh(0, t))
 
         for d in (1, 3, 2):
             reduce1(d).wait_recv()
@@ -429,9 +433,6 @@
         def _():
             y_pix(iy).wait_recv()
             z_pix.start()
-            z_mask.wait_recv()
-            s2_mask.start()
-            each(0, TILES, lambda t: weigh(2, t))
 
             @pl.when(iy == 1)
             def _():
@@ -441,10 +442,6 @@
             def _():
                 base(2)
 
-            s2_mask.wait_recv()
-            each(0, TILES, lambda t: weigh(0, t))
-
-        each(3, jnp.where(final, 3, Z_MARKS[0] - 1), z_send)
         for e in range(1, 8):
             reduce2(e).wait_recv()
         piece = sub(hp, j2)[...]
@@ -468,36 +465,41 @@
         for e in (2, 6, 4, 1, 7, 3, 5):
             gather2(e, j2).start()
         onward(j2)
-        y_more(y0 + 4, y0 + 10)
+        y_more(y0 + 3, y0 + 7)
 
         @pl.when(final)
         def _():
-            each(AHEAD + 2, CHUNKS, cross)
-
-        for e in (2, 6, 4, 1, 7, 3, 5):
+            each(AHEAD, AHEAD + 3, cross)
+            each(13, CHUNKS, y_send)
+
+        for n, e in enumerate((2, 6, 4, 1, 7, 3, 5)):
             j = (j2 + 8 - e) % 8
             gather2(e, j).wait_recv()
             onward(j)
+            if n == 3:
+
+                @pl.when(final)
+                def _():
+                    z_pix.wait_recv()
+
+                    @pl.when(iy == 2)
+                    def _():
+                        s2_pix.start()
+
+                    @pl.when(iy == 1)
+                    def _():
+                        set_halo(2)
+
+            if 3 <= n < 6:
+
+                @pl.when(final & (iy == 1))
+                def _():
+                    each(3 * n - 9, min(3 * n - 6, TILES), lambda t: base_tile(2, t))
 
         def pass_on(k, i, half):
             return rcopy(hf.at[half + k], hf.at[half + k], fs.at[i], fr.at[i], sibling)
 
         pass_on(q1, 0, mine).start()
-
-        @pl.when(final)
-        def _():
-            z_pix.wait_recv()
-
-            @pl.when(iy == 2)
-            def _():
-                s2_pix.start()
-
-            @pl.when(iy == 1)
-            def _():
-                base(2)
-
-            s2_pix.wait_recv()
-            base(0)
 
         def shift(t, accs):
             s_t = w[t] * mm(us[...], right(hf[t]))
@@ -533,11 +535,12 @@
             hand(i, i).wait_send()
             pass_on(i, i, mine).wait_send()
         def meanwhile():
-            y_more(y0 + 10, y0 + 13)
+            y_more(y0 + 7, y0 + 9)
 
             @pl.when(final)
             def _():
                 each(0, 2, halo_shift)
+                each(Z_MARKS[2] + 1, AHEAD, z_send)
                 ready(turn_of(0))
                 ready(turn_of(1))
 
@@ -547,26 +550,17 @@
 
             each(0, TILES, step)
 
-        def turn_shift(t):
-            lay[t] = jnp.transpose(hf[t])
-
         def early():
             @pl.when(final)
             def _():
-                each(0, TILES, turn_shift)
-
-        @pl.when(it == 0)
-        def _():
-            z_send(Z_MARKS[0] - 1)
-
+                s2_pix.wait_recv()
+                base(0)
+
+        z_send(jnp.where(final, Z_MARKS[2], Z_MARKS[0] - 1))
         sums = all_reduce(2 + 2 * it, pack(norm, *accs), meanwhile, early)
         step = sums[0:1] / sums[3:4]
         square = sums[1:2] - 2.0 * step * sums[2:3] + step * step * sums[3:4]
         lev[...] = jnp.broadcast_to(level_from(square), (8, 128))
-
-        @pl.when(final)
-        def _():
-            each(Z_MARKS[2], AHEAD, z_send)
 
         inverse = 1.0 / level_from(square)
 
@@ -581,7 +575,6 @@
             def _():
                 ya[t, inner, :] = soft(r_t * inverse)
                 s1_layer(t).start()
-                vio[t] = vio[t] + step * lay[t]
 
         each(0, TILES, update)
         lev2[...] = jnp.broadcast_to(step, (8, 128))
@@ -640,6 +633,7 @@
             yb[t, rows, :] = own + diffusion * (g(y_sib[t, pl.ds(at, STRIP), :] - own) + to1 + net(0, at))
             p_far[t, pl.ds(at, STRIP), :] = y1 + diffusion * (g(has2 * (halo(1, at) - y1)) - to1 + net(1, at))
         s1_pass(t).start()
+        vio[t] = jnp.transpose(vt[t])
 
     def pass2(t):
         along(yb.at[t], fb.at[2])

time: 172 us -> 168 us (0.977)
  Pallas kernels: 172 us -> 167 us
    pallas_call x1, Pallas kernels: 169 us -> 165 us  [per_device(): pl.pallas_call(kernel, out_shape=(pltpu.VMEM((TILE, TILE), f32), pltpu.VM...]
where the time goes in v5:
time: 168 us
  Pallas kernels  167 us (99%)
    pallas_call x1, Pallas kernels, per_device(): pl.pallas_call(kernel, out_shape=(pltpu.VMEM((TILE, TILE), f32), pltpu.VM...  165 us

profile of v5, /device:TPU:1, one launch (start us, length us, event | category | flops | bytes accessed | tf_op | source)
XLA Modules:
  0.0 167.9 jit_solution(8198011350622787888)
XLA Ops:
  0.6 165.1 %separate.1 = (f32[256,256]{1,0:T(8,128)S(1)}, f32[8,256,256]{2,1,0:T(8,128)S(1)}, f32[8,256,256]{2,1,0:T(8,128)S(1)}) custom-call(f32[256,2048]{1,0:T(8,128)} %obs_in.1, s32[256,256]{1,0:T(8,128)} %mask_in.1, f32[256,256]{1,0:T(8,128)} %u_in.1, f32[2048,256]{1,0:T(8,128)} %v_in.1), custom_call_target="tpu_custom_call" | custom-call | tf_op jit(solution)/shard_map/separate/pallas_call | solution.py:713
  165.7 2.2 %hand_out.1 = (f32[256,256]{1,0:T(8,128)}, f32[2048,256]{1,0:T(8,128)}, f32[256,2048]{1,0:T(8,128)}) custom-call(f32[256,256]{1,0:T(8,128)S(1)} %get-tuple-element.6.u_in, f32[8,256,256]{2,1,0:T(8,128)S(1)} %get-tuple-element.7.v_in, f32[8,256,256]{2,1,0:T(8,128)S(1)} %get-tuple-element.8.c_in), custom_call_target="tpu_custom_call" | custom-call | tf_op jit(solution)/shard_map/hand_out/pallas_call | solution.py:767

commit v6 on v5

--- a/solution.py
+++ b/solution.py
@@ -11,7 +11,7 @@
 TILE = 256
 TILES = 8
 CHUNKS = 16
-Z_MARKS = (4, 5, 8)
+Z_MARKS = (4, 4, 8)
 AHEAD = 11
 
 TOTAL = 67108864.0
@@ -194,9 +194,13 @@
         vt[t] = vt_t
         vs[t] = right(vt_t)
 
-    each(0, TILES, turn_v)
-    for load in loads[TILES:]:
+    turn_v(0)
+    for load in loads[TILES : TILES + 2]:
         load.wait()
+
+    def obs_load(t):
+        cols = pl.ds(pl.multiple_of(t * TILE, TILE), TILE)
+        return pltpu.make_async_copy(obs_in.at[:, cols], r.at[t], in_sem.at[TILES + 2 + t])
 
     def set_u(value):
         u[...] = value
@@ -209,10 +213,12 @@
         return mm(dates, spread[t % 4])
 
     def first(t, acc):
+        obs_load(t).wait()
         w_t = weight(mask, t)
         w[t] = w_t
         r_t = w_t * (r[t] - mm(us[...], vs[t]))
         r[t] = r_t
+        turn_v(jnp.minimum(t + 1, TILES - 1))
         return acc + fold(r_t * r_t)
 
     zero = jnp.zeros((8, 128), f32)
@@ -458,7 +464,7 @@
             return rcopy(hf.at[mine + k], hf.at[mine + k], a1s.at[d - 1], a1r.at[d - 1], ring1((q1 + d) % 4))
 
         def onward(j):
-            for d in (2, 1, 3):
+            for d in (1, 3, 2):
                 piece = sub(hf, j)
                 rcopy(piece, piece, a1s.at[d - 1], a1r.at[d - 1], ring1((q1 + d) % 4)).start()
 
@@ -525,15 +531,6 @@
 
         accs = lax.fori_loop(1, 4, shift_step, shift(mine + q1, (zero, zero, zero)))
         accs = shift_other(3, accs)
-        for d in (1, 2, 3):
-            reduce1(d).wait_send()
-            gather1(d, q1).wait_send()
-        for e in range(1, 8):
-            reduce2(e).wait_send()
-            gather2(e, j2).wait_send()
-        for i in range(4):
-            hand(i, i).wait_send()
-            pass_on(i, i, mine).wait_send()
         def meanwhile():
             y_more(y0 + 7, y0 + 9)
 
@@ -551,8 +548,22 @@
             each(0, TILES, step)
 
         def early():
+            for d in (1, 2, 3):
+                reduce1(d).wait_send()
+                gather1(d, q1).wait_send()
+            for e in range(1, 8):
+                reduce2(e).wait_send()
+                gather2(e, j2).wait_send()
+            for i in range(4):
+                hand(i, i).wait_send()
+                pass_on(i, i, mine).wait_send()
+
             @pl.when(final)
             def _():
+                y_mask(iz).wait_send()
+                y_pix(iz).wait_send()
+                each(0, CHUNKS, lambda i: y_obs(i, iz).wait_send())
+                each(AHEAD, CHUNKS, lambda i: ahead(i).wait_send())
                 s2_pix.wait_recv()
                 base(0)
 
@@ -660,24 +671,14 @@
     for row in range(3):
         fb[row, :AT, :] = jnp.zeros((AT, TILE), f32)
     each(0, TILES + 2, smooth_tile)
-    y_mask(iz).wait_send()
-    y_pix(iz).wait_send()
     for copy in (z_mask, z_pix, s2_mask, s2_pix):
         copy.wait_send()
 
     def drain(i):
-        y_obs(i, iz).wait_send()
-
-        @pl.when(i < AHEAD)
-        def _():
-            z_obs(i).wait_send()
-
-        @pl.when(i >= AHEAD)
-        def _():
-            ahead(i).wait_send()
-            across(i, iy).wait_send()
-
-    each(0, CHUNKS, drain)
+        z_obs(i).wait_send()
+
+    each(0, AHEAD, drain)
+    each(AHEAD, CHUNKS, lambda i: across(i, iy).wait_send())
 
     def close(t):
         s1_layer(t).wait_send()

time: 168 us -> 167 us (level)
  no operation moved by 1% of the time
where the time goes in v6:
time: 167 us
  Pallas kernels  166 us (99%)
    pallas_call x1, Pallas kernels, per_device(): pl.pallas_call(kernel, out_shape=(pltpu.VMEM((TILE, TILE), f32), pltpu.VM...  164 us

profile of v6, /device:TPU:1, one launch (start us, length us, event | category | flops | bytes accessed | tf_op | source)
XLA Modules:
  0.0 166.6 jit_solution(16714737353984664443)
XLA Ops:
  0.6 163.8 %separate.1 = (f32[256,256]{1,0:T(8,128)S(1)}, f32[8,256,256]{2,1,0:T(8,128)S(1)}, f32[8,256,256]{2,1,0:T(8,128)S(1)}) custom-call(f32[256,2048]{1,0:T(8,128)} %obs_in.1, s32[256,256]{1,0:T(8,128)} %mask_in.1, f32[256,256]{1,0:T(8,128)} %u_in.1, f32[2048,256]{1,0:T(8,128)} %v_in.1), custom_call_target="tpu_custom_call" | custom-call | tf_op jit(solution)/shard_map/separate/pallas_call | solution.py:714
  164.4 2.2 %hand_out.1 = (f32[256,256]{1,0:T(8,128)}, f32[2048,256]{1,0:T(8,128)}, f32[256,2048]{1,0:T(8,128)}) custom-call(f32[256,256]{1,0:T(8,128)S(1)} %get-tuple-element.6.u_in, f32[8,256,256]{2,1,0:T(8,128)S(1)} %get-tuple-element.7.v_in, f32[8,256,256]{2,1,0:T(8,128)S(1)} %get-tuple-element.8.c_in), custom_call_target="tpu_custom_call" | custom-call | tf_op jit(solution)/shard_map/hand_out/pallas_call | solution.py:768

commit v7 on v6

--- a/solution.py
+++ b/solution.py
@@ -471,7 +471,7 @@
         for e in (2, 6, 4, 1, 7, 3, 5):
             gather2(e, j2).start()
         onward(j2)
-        y_more(y0 + 3, y0 + 7)
+        y_more(y0 + 3, y0 + 6)
 
         @pl.when(final)
         def _():
@@ -532,7 +532,7 @@
         accs = lax.fori_loop(1, 4, shift_step, shift(mine + q1, (zero, zero, zero)))
         accs = shift_other(3, accs)
         def meanwhile():
-            y_more(y0 + 7, y0 + 9)
+            y_more(y0 + 6, y0 + 9)
 
             @pl.when(final)
             def _():

time: 167 us -> 167 us (level)
  no operation moved by 1% of the time
where the time goes in v7:
time: 167 us
  Pallas kernels  166 us (99%)
    pallas_call x1, Pallas kernels, per_device(): pl.pallas_call(kernel, out_shape=(pltpu.VMEM((TILE, TILE), f32), pltpu.VM...  164 us

profile of v7, /device:TPU:1, one launch (start us, length us, event | category | flops | bytes accessed | tf_op | source)
XLA Modules:
  0.0 166.8 jit_solution(7073089507425514125)
XLA Ops:
  0.6 163.9 %separate.1 = (f32[256,256]{1,0:T(8,128)S(1)}, f32[8,256,256]{2,1,0:T(8,128)S(1)}, f32[8,256,256]{2,1,0:T(8,128)S(1)}) custom-call(f32[256,2048]{1,0:T(8,128)} %obs_in.1, s32[256,256]{1,0:T(8,128)} %mask_in.1, f32[256,256]{1,0:T(8,128)} %u_in.1, f32[2048,256]{1,0:T(8,128)} %v_in.1), custom_call_target="tpu_custom_call" | custom-call | tf_op jit(solution)/shard_map/separate/pallas_call | solution.py:714
  164.5 2.2 %hand_out.1 = (f32[256,256]{1,0:T(8,128)}, f32[2048,256]{1,0:T(8,128)}, f32[256,2048]{1,0:T(8,128)}) custom-call(f32[256,256]{1,0:T(8,128)S(1)} %get-tuple-element.6.u_in, f32[8,256,256]{2,1,0:T(8,128)S(1)} %get-tuple-element.7.v_in, f32[8,256,256]{2,1,0:T(8,128)S(1)} %get-tuple-element.8.c_in), custom_call_target="tpu_custom_call" | custom-call | tf_op jit(solution)/shard_map/hand_out/pallas_call | solution.py:768
